TPU v7x, 32 devices: a whole 2x2x4 slice. The times are simulated.
32 devices in a mesh: grp: 2 (over x), row: 16 (over z, y, core).
Axes of the slice: x: 2, y: 2, z: 4, core: 2. Of those that a mesh axis runs over, the one named last changes fastest.
Arguments:
- patches: bfloat16 [256, 32, 512], P(('grp', 'row')), parts along dimension 0, may hold values from -6 to 6
- registers: float32 [512, 512], P(('grp', 'row')), parts along dimension 0, may hold values from -6 to 6
- gain_one: float32 [512], replicated, may hold values from 0.1 to 1.9
- gain_two: float32 [512], replicated, may hold values from 0.1 to 1.9
- w_qkv_one: bfloat16 [512, 1536], replicated, may hold values from -4 to 4, as said below
- w_out_one: bfloat16 [512, 512], replicated, may hold values from -0.25 to 0.25
- w_qkv_two: bfloat16 [512, 1536], replicated, may hold values from -4 to 4, as said below
- w_out_two: bfloat16 [512, 512], replicated, may hold values from -0.25 to 0.25
Outputs:
- patches_out: bfloat16 [256, 32, 512], P(('grp', 'row')), parts along dimension 0
- registers_out: float32 [512, 512], P(('grp', 'row')), parts along dimension 0
There are 2 independent parts, one for each index of `grp`. A program takes and returns all parts, laid end to end along the dimension named above; an argument that names none is the same for every part. Nothing has to cross between parts.
Inputs may be any that keep to these rules, and one draw needn't show every extreme that they name: `w_qkv_one`: projection weights of the query, key and value columns. `w_qkv_two`: projection weights of the query, key and value columns.
All inputs are finite; a program needn't handle non-finite values.
Results may differ from a plain program's by a relative error of at most 0.01.
Values may be sent and summed in bfloat16 or wider, within the bound.
No kernel may reach another device: no remote copies, remote signals or barrier semaphores. Data moves between devices by JAX's collectives and lax.ppermute only.
A program may use at most 128 MiB of HBM per device.

v0:
```python
import math

import jax
import jax.numpy as jnp
from jax import lax
from jax.sharding import PartitionSpec as P

HEADS = 16
WIN = 8
REG = 16


def layer_norm(values, gain):
    values = values.astype(jnp.float32)
    mean = jnp.mean(values, -1, keepdims=True)
    centred = values - mean
    spread = jnp.mean(centred * centred, -1, keepdims=True)
    return centred * lax.rsqrt(spread + 1e-05) * gain


def attend(query, keys, values):
    count, qlen, width = query.shape
    hdim = width // HEADS
    q_heads = query.reshape(count, qlen, HEADS, hdim)
    k_heads = keys.reshape(count, keys.shape[1], HEADS, hdim)
    v_heads = values.reshape(count, keys.shape[1], HEADS, hdim)
    scores = jnp.einsum(
        "nqhe,nkhe->nhqk", q_heads, k_heads, preferred_element_type=jnp.float32
    ) / math.sqrt(hdim)
    top = jnp.max(scores, -1, keepdims=True)
    expo = jnp.exp(scores - top)
    weights = (expo / jnp.sum(expo, -1, keepdims=True)).astype(jnp.bfloat16)
    result = jnp.einsum("nhqk,nkhe->nqhe", weights, v_heads, preferred_element_type=jnp.float32)
    return result.reshape(count, qlen, width).astype(jnp.bfloat16)


def on_device(patches, registers, gain_one, gain_two, w_qkv_one, w_out_one, w_qkv_two, w_out_two):
    rows, width, dim = patches.shape
    nrow = lax.axis_size("row")
    per_band = nrow // 8
    cls = width // WIN
    groups = nrow // cls
    sub_rows = rows // groups
    normed = layer_norm(patches, gain_one).astype(jnp.bfloat16)
    qkv = jnp.dot(normed.reshape(-1, dim), w_qkv_one, preferred_element_type=jnp.float32).astype(
        jnp.bfloat16
    )
    qkv = qkv.reshape(rows, width, 3 * dim)
    reg_normed = layer_norm(registers, gain_one).astype(jnp.bfloat16)
    reg_qkv = jnp.dot(reg_normed, w_qkv_one, preferred_element_type=jnp.float32).astype(
        jnp.bfloat16
    )
    count = width // WIN
    tiles = (
        qkv.reshape(rows, count, WIN, 3 * dim)
        .transpose(1, 0, 2, 3)
        .reshape(count, rows * WIN, 3 * dim)
    )
    reg_side = jnp.broadcast_to(reg_qkv[None, :, dim:], (count, REG, 2 * dim))
    keys_all = jnp.concatenate([tiles[:, :, dim:], reg_side], 1)
    block = attend(tiles[:, :, :dim], keys_all[:, :, :dim], keys_all[:, :, dim:])
    block = block.reshape(count, rows, WIN, dim).transpose(1, 0, 2, 3).reshape(rows * width, dim)
    block_out = (
        patches.reshape(-1, dim).astype(jnp.float32)
        + jnp.dot(block, w_out_one, preferred_element_type=jnp.float32)
    ).astype(jnp.bfloat16)
    block_out = block_out.reshape(rows, width, dim)
    band_keys = jnp.concatenate(
        [qkv.reshape(1, rows * width, 3 * dim)[:, :, dim:], reg_qkv[None, :, dim:]], 1
    )
    reg_att = attend(reg_qkv[None, :, :dim], band_keys[:, :, :dim], band_keys[:, :, dim:])[0]
    reg_out = registers + jnp.dot(reg_att, w_out_one, preferred_element_type=jnp.float32)
    reg_normed_two = layer_norm(reg_out, gain_two).astype(jnp.bfloat16)
    own_kv = jnp.dot(reg_normed_two, w_qkv_two[:, dim:], preferred_element_type=jnp.float32).astype(
        jnp.bfloat16
    )
    reg_kv = lax.all_gather(own_kv, "row", axis=0, tiled=True)
    grouped = (
        reg_kv.reshape(WIN, per_band, REG, 2 * dim)
        .transpose(1, 0, 2, 3)
        .reshape(per_band, WIN * REG, 2 * dim)
    )
    normed_two = layer_norm(block_out, gain_two).astype(jnp.bfloat16)
    projected = jnp.dot(
        normed_two.reshape(-1, dim), w_qkv_two, preferred_element_type=jnp.float32
    ).astype(jnp.bfloat16)
    projected = projected.reshape(rows, width, 3 * dim)
    last = projected.shape[-1]
    values = lax.all_to_all(
        projected.reshape(groups, sub_rows, WIN, cls, last)
        .transpose(0, 3, 1, 2, 4)
        .reshape(groups * cls, sub_rows, WIN, last),
        "row",
        split_axis=0,
        concat_axis=0,
        tiled=True,
    )
    nitems = values.shape[1]
    grid_last = values.shape[-1]
    windows = values.reshape(WIN, per_band, nitems, WIN, grid_last).transpose(1, 2, 0, 3, 4)
    windows, nitems = (windows.reshape(per_band * nitems, WIN * WIN, grid_last), nitems)
    regs = jnp.broadcast_to(grouped[:, None], (per_band, nitems, WIN * REG, 2 * dim))
    regs = regs.reshape(per_band * nitems, WIN * REG, 2 * dim)
    full_keys = jnp.concatenate([windows[:, :, dim : 2 * dim], regs[:, :, :dim]], 1)
    full_vals = jnp.concatenate([windows[:, :, 2 * dim :], regs[:, :, dim:]], 1)
    att = attend(windows[:, :, :dim], full_keys, full_vals)
    last = att.shape[-1]
    shaped = att.reshape(per_band, nitems, WIN, WIN, last).transpose(2, 0, 1, 3, 4)
    finished = shaped.reshape(nrow, nitems, WIN, last)
    values = lax.all_to_all(finished, "row", split_axis=0, concat_axis=0, tiled=True)
    last = values.shape[-1]
    home = (
        values.reshape(groups, cls, sub_rows, WIN, last)
        .transpose(0, 2, 3, 1, 4)
        .reshape(rows, width, last)
    )
    patches_out = (
        block_out.reshape(-1, dim).astype(jnp.float32)
        + jnp.dot(home.reshape(-1, dim), w_out_two, preferred_element_type=jnp.float32)
    ).astype(jnp.bfloat16)
    patches_out = patches_out.reshape(rows, width, dim)
    return (patches_out, reg_out)


def solution(mesh):
    in_specs = (
        P(("grp", "row"), None, None),
        P(("grp", "row"), None),
        P(),
        P(),
        P(),
        P(),
        P(),
        P(),
    )
    out_specs = (P(("grp", "row"), None, None), P(("grp", "row"), None))
    return jax.shard_map(
        on_device, mesh=mesh, in_specs=in_specs, out_specs=out_specs, check_vma=False
    )
```

profile of v0, /device:TPU:0, one launch (start us, length us, event | category | flops | bytes accessed | tf_op | source)
XLA Modules:
  0.0 103.5 jit_solution(9667902232440209475)
XLA Ops:
  0.6 0.0 copy-start
  0.6 1.2 %convert_reduce_fusion = f32[8,32]{1,0:T(8,128)S(1)} fusion(bf16[8,32,512]{2,1,0:T(8,128)(2,1)} %param.8), kind=kLoop, calls=%fused_computation.45 | loop fusion | flops 261888 | bytes 263168 | tf_op jit(solution)/shard_map/reduce_sum | solution.py:15
  1.8 1.2 %multiply_reduce_fusion.3 = f32[8,32]{1,0:T(8,128)S(1)} fusion(bf16[8,32,512]{2,1,0:T(8,128)(2,1)} %param.8, f32[8,32]{1,0:T(8,128)S(1)} %broadcast_multiply_fusion), kind=kLoop, calls=%fused_computation.44 | loop fusion | flops 524032 | bytes 264192 | tf_op jit(solution)/shard_map/reduce_sum | solution.py:17
  3.0 1.1 %multiply_convert_fusion.1 = bf16[8,32,512]{2,1,0:T(8,128)(2,1)S(1)} fusion(bf16[8,32,512]{2,1,0:T(8,128)(2,1)} %param.8, f32[512]{0:T(512)} %param.10, f32[8,32]{1,0:T(8,128)S(1)} %add_rsqrt_fusion, f32[8,32]{1,0:T(8,128)S(1)} %broadcast_multiply_fusion), kind=kLoop, calls=%fused_computation.43 | loop fusion | flops 655360 | bytes 528384 | tf_op jit(solution)/shard_map/convert_element_type | solution.py:44
  4.1 0.0 copy-done
  4.1 0.6 convolution_convert_fusion.1
  4.7 0.0 copy-start.5
  4.7 0.0 copy-start.7
  4.8 0.1 copy.40
  4.8 0.7 slice.65
  5.5 0.1 slice.61
  5.6 0.0 copy-done.5
  5.6 0.1 reduce_sum.101
  5.7 0.2 multiply_reduce_fusion.5
  5.9 0.4 convolution_convert_fusion.2
  6.3 0.9 pad_maximum_fusion.2
  7.2 1.2 %copy.17 = bf16[4,80,512]{1,2,0:T(8,128)(2,1)S(1)} copy(bf16[4,80,512]{2,1,0:T(8,128)(2,1)} %get-tuple-element.7) | data formatting | bytes 655360 | tf_op jit(solution)/shard_map/slice | solution.py:61
  8.5 1.2 %copy.16 = bf16[4,64,512]{1,2,0:T(8,128)(2,1)S(1)} copy(bf16[4,64,512]{2,1,0:T(8,128)(2,1)} %slice.65) | data formatting | bytes 524288 | tf_op jit(solution)/shard_map/slice | solution.py:61
  9.7 2.0 %copy.15 = bf16[4,80,512]{1,2,0:T(8,128)(2,1)} copy(bf16[4,80,512]{2,1,0:T(8,128)(2,1)} %get-tuple-element.8) | data formatting | bytes 655360 | tf_op jit(solution)/shard_map/slice | solution.py:61
  11.7 2.9 %fusion.41 = (f32[4,16,64]{2,1,0:T(8,128)}, f32[4,16,64,80]{3,2,1,0:T(8,128)}) fusion(bf16[4,64,16,32]{1,3,2,0:T(8,128)(2,1)S(1)} %bitcast.84, bf16[4,80,16,32]{1,3,2,0:T(8,128)(2,1)S(1)} %bitcast.85), kind=kOutput, calls=%fused_computation.82 | convolution fusion | flops 21954640 | bytes 1916928 | tf_op jit(solution)/shard_map/sub | solution.py:31
  14.6 2.4 %fusion.12 = bf16[4,64,16,32]{1,3,2,0:T(8,128)(2,1)S(1)} fusion(bf16[4,80,16,32]{1,3,2,0:T(8,128)(2,1)} %bitcast.98, f32[4,16,64,80]{3,2,1,0:T(8,128)} %get-tuple-element.14, f32[4,16,64]{2,1,0:T(8,128)} %get-tuple-element.13), kind=kOutput, calls=%fused_computation.20 | convolution fusion | flops 21757952 | bytes 1916928 | tf_op jit(solution)/shard_map/nhqk,nkhe->nqhe/dot_general | solution.py:33
  17.0 0.0 copy-start.2
  17.0 1.7 %copy.18 = bf16[4,64,16,32]{3,2,1,0:T(8,128)(2,1)} copy(bf16[4,64,16,32]{1,3,2,0:T(8,128)(2,1)S(1)} %fusion.12) | data formatting | bytes 524288 | tf_op jit(solution)/shard_map/convert_element_type | solution.py:34
  18.8 2.2 %convert_element_type.102 = bf16[4,8,8,512]{3,2,1,0:T(8,128)(2,1)S(1)} reshape(bf16[4,64,16,32]{3,2,1,0:T(8,128)(2,1)} %copy.18) | data formatting | bytes 524288 | tf_op jit(solution)/shard_map/convert_element_type | solution.py:34
  21.0 0.0 copy-start.1
  21.0 1.5 %fusion.44 = (f32[256]{0:T(256)S(1)}, f32[256,512]{1,0:T(8,128)S(1)}) fusion(bf16[256,512]{1,0:T(8,128)(2,1)S(1)} %bitcast.96, bf16[512,512]{1,0:T(8,128)(2,1)} %param.13, bf16[256,512]{1,0:T(8,128)(2,1)S(1)} %bitcast.78), kind=kOutput, calls=%fused_computation.85 | convolution fusion | flops 134872832 | bytes 1573888 | tf_op jit(solution)/shard_map/dot_general | solution.py:65
  22.6 0.2 multiply_reduce_fusion.2
  22.8 1.5 %convolution_convert_fusion = bf16[256,1536]{1,0:T(8,128)(2,1)} fusion(bf16[512,1536]{1,0:T(8,128)(2,1)S(1)} %copy-done.1, f32[256,512]{1,0:T(8,128)S(1)} %get-tuple-element.20, f32[512]{0:T(512)S(1)} %copy-done.8, f32[256]{0:T(256)S(1)} %add_rsqrt_fusion.1, f32[256]{0:T(256)S(1)} %broadcast_multiply_fusion.1), kind=kOutput, calls=%fused_computation.7 | convolution fusion | flops 403570688 | bytes 2887680 | tf_op jit(solution)/shard_map/dot_general | solution.py:84
  24.3 2.4 %reshape_reshape.13 = bf16[4,2,8,4,1536]{4,3,2,1,0:T(4,128)(2,1)} reshape(bf16[256,1536]{1,0:T(8,128)(2,1)} %convolution_convert_fusion) | data formatting | bytes 1572864 | tf_op jit(solution)/shard_map/reshape;reshape | solution.py:90
  26.7 2.2 %copy.20 = bf16[4,2,8,4,1536]{4,2,1,3,0:T(8,128)(2,1)} copy(bf16[4,2,8,4,1536]{4,3,2,1,0:T(4,128)(2,1)} %reshape_reshape.13) | data formatting | bytes 1572864 | tf_op jit(solution)/shard_map/reshape;reshape | solution.py:90
  28.9 7.5 %all-to-all-start = ((bf16[16,2,8,1536]{3,2,1,0:T(8,128)(2,1)}), bf16[16,2,8,1536]{3,2,1,0:T(8,128)(2,1)}, u32[]{:S(2)}, u32[]{:S(2)}) async-start(bf16[16,2,8,1536]{3,2,1,0:T(8,128)(2,1)} %bitcast.80), calls=%async_computation | async-start | bytes 1572864 | tf_op jit(solution)/shard_map/all_to_all | solution.py:89
  36.4 0.1 reshape.188
  36.5 0.1 slice.67
  36.5 0.8 pad_maximum_fusion.3
  37.3 1.2 %copy.23 = bf16[1,272,512]{1,2,0:T(8,128)(2,1)S(1)} copy(bf16[1,272,512]{2,1,0:T(8,128)(2,1)} %get-tuple-element.9) | data formatting | bytes 557056 | tf_op jit(solution)/shard_map/slice | solution.py:71
  38.5 0.9 copy.22
  39.4 0.4 fusion.42
  39.8 1.3 %fusion.17 = bf16[1,16,16,32]{3,1,2,0:T(8,128)(2,1)S(1)} fusion(bf16[272,16,32]{0,2,1:T(8,128)(2,1)} %bitcast.99, f32[16,16,272]{2,1,0:T(8,128)S(1)} %get-tuple-element.16, f32[16,16]{1,0:T(8,128)S(1)} %get-tuple-element.15), kind=kOutput, calls=%fused_computation.29 | convolution fusion | flops 4603904 | bytes 574464 | tf_op jit(solution)/shard_map/nhqk,nkhe->nqhe/dot_general | solution.py:33
  41.2 0.1 convert_element_type.111
  41.3 0.3 fusion.43
  41.6 0.0 copy-start.6
  41.6 0.2 multiply_reduce_fusion.4
  41.8 1.5 %convolution_convert_fusion.5 = bf16[16,1024]{1,0:T(8,128)(2,1)S(1)} fusion(bf16[512,1536]{1,0:T(8,128)(2,1)} %param.14, f32[16,512]{1,0:T(8,128)S(1)} %get-tuple-element.18, f32[512]{0:T(512)S(1)} %copy-done.8, f32[16]{0:T(128)S(1)} %add_rsqrt_fusion.2, f32[16]{0:T(128)S(1)} %broadcast_multiply_fusion.2), kind=kOutput, calls=%fused_computation.30 | convolution fusion | flops 16826368 | bytes 1116288 | tf_op jit(solution)/shard_map/dot_general | solution.py:74
  43.3 24.1 %all_gather.3 = bf16[256,1024]{1,0:T(8,128)(2,1)S(1)} all-gather(bf16[16,1024]{1,0:T(8,128)(2,1)S(1)} %convolution_convert_fusion.5), channel_id=1, replica_groups=mesh['grp'=2,'row'=16] {'row'}, dimensions={0}, use_global_device_ids=true | all-gather | bytes 557056 | tf_op jit(solution)/shard_map/all_gather | solution.py:77
  67.5 0.3 copy.27
  67.8 0.1 broadcast_in_dim.11
  67.9 1.0 %fusion.39 = (bf16[4,128,512]{1,2,0:T(8,128)(2,1)}, bf16[4,128,512]{1,2,0:T(8,128)(2,1)}) fusion(bf16[4,128,1024]{1,2,0:T(8,128)(2,1)S(1)} %bitcast.77), kind=kLoop, calls=%fused_computation.80 | loop fusion | bytes 2097152 | tf_op jit(solution)/shard_map/slice | solution.py:104
  69.0 0.0 all-to-all-done
  69.0 1.2 %copy.21 = bf16[2,2,8,8,1536]{4,3,2,1,0:T(8,128)(2,1)S(1)} copy(bf16[2,2,8,8,1536]{4,3,1,0,2:T(8,128)(2,1)} %bitcast.15) | data formatting | bytes 1572864 | tf_op jit(solution)/shard_map/transpose | solution.py:100
  70.2 0.1 fusion.40
  70.2 1.0 copy.30
  71.2 1.0 copy.29
  72.3 1.0 copy.28
  73.3 3.3 %pad_maximum_fusion = (bf16[4,192,512]{1,2,0:T(8,128)(2,1)}, bf16[4,192,512]{1,2,0:T(8,128)(2,1)S(1)}) fusion(bf16[4,128,512]{1,2,0:T(8,128)(2,1)} %get-tuple-element.3, bf16[4,64,512]{1,2,0:T(8,128)(2,1)} %copy.28, bf16[4,128,512]{1,2,0:T(8,128)(2,1)} %get-tuple-element.2, bf16[4,64,512]{1,2,0:T(8,128)(2,1)} %copy.30), kind=kLoop, calls=%fused_computation.32 | loop fusion | flops 3145728 | bytes 3145728 | tf_op jit(solution)/shard_map/concatenate | solution.py:105
  76.6 4.4 %fusion.45 = (f32[4,16,64]{2,1,0:T(8,128)S(1)}, f32[4,16,64,192]{3,2,1,0:T(8,128)}) fusion(bf16[4,64,16,32]{1,3,2,0:T(8,128)(2,1)} %bitcast.88, bf16[4,192,16,32]{1,3,2,0:T(8,128)(2,1)S(1)} %bitcast.79), kind=kOutput, calls=%fused_computation.86 | convolution fusion | flops 52691136 | bytes 4210688 | tf_op jit(solution)/shard_map/sub | solution.py:31
  81.0 4.1 %fusion.11 = bf16[4,64,16,32]{1,3,2,0:T(8,128)(2,1)} fusion(bf16[4,192,16,32]{1,3,2,0:T(8,128)(2,1)} %bitcast.97, f32[4,16,64,192]{3,2,1,0:T(8,128)} %get-tuple-element.22, f32[4,16,64]{2,1,0:T(8,128)S(1)} %get-tuple-element.21), kind=kOutput, calls=%fused_computation.19 | convolution fusion | flops 52035584 | bytes 4210688 | tf_op jit(solution)/shard_map/nhqk,nkhe->nqhe/dot_general | solution.py:33
  85.1 1.8 %copy.31 = bf16[4,64,16,32]{3,2,1,0:T(8,128)(2,1)S(1)} copy(bf16[4,64,16,32]{1,3,2,0:T(8,128)(2,1)} %fusion.11) | data formatting | bytes 524288 | tf_op jit(solution)/shard_map/convert_element_type | solution.py:34
  86.9 1.0 convert_element_type.117
  87.9 0.0 copy-start.4
  88.0 14.3 %all_to_all.10 = bf16[16,2,8,512]{3,2,1,0:T(8,128)(2,1)S(1)} all-to-all(bf16[16,2,8,512]{3,2,1,0:T(8,128)(2,1)S(1)} %bitcast.93), channel_id=1, replica_groups=mesh['grp'=2,'row'=16] {'row'}, dimensions={0} | all-to-all | bytes 524288 | tf_op jit(solution)/shard_map/all_to_all | solution.py:110
  102.2 0.2 copy.41
  102.5 0.1 reshape_reshape.15
  102.5 0.0 copy-done.4
  102.5 1.0 fusion.15
  (23 shorter events, 0.2 us)
Async XLA Ops:
  0.6 3.5 %copy-start = (bf16[512,1536]{1,0:T(8,128)(2,1)S(1)}, bf16[512,1536]{1,0:T(8,128)(2,1)}, u32[]{:S(2)}) copy-start(bf16[512,1536]{1,0:T(8,128)(2,1)} %param.12) | copy-start | bytes 4718596
  4.7 0.9 copy-start.5
  4.7 1.2 %copy-start.7 = (f32[512]{0:T(512)S(1)}, f32[512]{0:T(512)}, u32[]{:S(2)}) copy-start(f32[512]{0:T(512)} %param.10) | copy-start | bytes 6148
  17.0 4.0 %copy-start.2 = (bf16[8,32,512]{2,1,0:T(8,128)(2,1)S(1)}, bf16[8,32,512]{2,1,0:T(8,128)(2,1)}, u32[]{:S(2)}) copy-start(bf16[8,32,512]{2,1,0:T(8,128)(2,1)} %param.8) | copy-start | bytes 786436
  18.8 4.1 %copy-start.8 = (f32[512]{0:T(512)S(1)}, f32[512]{0:T(512)}, u32[]{:S(2)}) copy-start(f32[512]{0:T(512)} %param.11) | copy-start | bytes 6148
  21.0 1.8 %copy-start.1 = (bf16[512,1536]{1,0:T(8,128)(2,1)S(1)}, bf16[512,1536]{1,0:T(8,128)(2,1)}, u32[]{:S(2)}) copy-start(bf16[512,1536]{1,0:T(8,128)(2,1)} %param.14) | copy-start | bytes 4718596
  28.9 40.1 %all-to-all-start = ((bf16[16,2,8,1536]{3,2,1,0:T(8,128)(2,1)}), bf16[16,2,8,1536]{3,2,1,0:T(8,128)(2,1)}, u32[]{:S(2)}, u32[]{:S(2)}) async-start(bf16[16,2,8,1536]{3,2,1,0:T(8,128)(2,1)} %bitcast.80), calls=%async_computation | async-start | bytes 1572864 | tf_op jit(solution)/shard_map/all_to_all | solution.py:89
  37.3 4.0 %copy-start.3 = (bf16[512,512]{1,0:T(8,128)(2,1)S(1)}, bf16[512,512]{1,0:T(8,128)(2,1)}, u32[]{:S(2)}) copy-start(bf16[512,512]{1,0:T(8,128)(2,1)} %param.13) | copy-start | bytes 1572868
  41.6 26.3 %copy-start.6 = (f32[16,512]{1,0:T(8,128)}, f32[16,512]{1,0:T(8,128)S(1)}, u32[]{:S(2)}) copy-start(f32[16,512]{1,0:T(8,128)S(1)} %get-tuple-element.18) | copy-start | bytes 98308
  87.9 14.6 %copy-start.4 = (bf16[512,512]{1,0:T(8,128)(2,1)S(1)}, bf16[512,512]{1,0:T(8,128)(2,1)}, u32[]{:S(2)}) copy-start(bf16[512,512]{1,0:T(8,128)(2,1)} %param.15) | copy-start | bytes 1572868
where the time goes:
time: 104 us
  blocking collectives  38.4 us (37%)
  local copies, waits for them, and re-layouts  25.2 us (24%)
  matrix products  22.3 us (21%)
  other arithmetic  9.17 us (9%)
  starting transfers between devices  7.46 us (7%)
    all_gather x1, blocking collectives, on_device(): reg_kv = lax.all_gather(own_kv, 'row', axis=0, tiled=True)  24.1 us
    all_to_all x1, blocking collectives, on_device(): lax.all_to_all(finished, 'row', split_axis=0, concat_axis=0, tiled=True)  14.3 us
    dot_general x3, matrix products, attend(): jnp.einsum('nhqk,nkhe->nqhe', weights, v_heads, preferred_element_type=jn...  7.81 us
    sub x3, matrix products, attend(): expo = jnp.exp(scores - top)  7.69 us
    all_to_all x1, starting transfers between devices, on_device(): lax.all_to_all(projected.reshape(groups, sub_rows, WIN, cls, last).transp...  7.46 us
    convert_element_type x6, local copies, waits for them, and re-layouts, attend(): return result.reshape(count, qlen, width).astype(jnp.bfloat16)  6.92 us
    another operation x2, local copies, waits for them, and re-layouts, on_device(): projected.reshape(groups, sub_rows, WIN, cls, last).transpose(0, 3, 1, 2, 4)  4.55 us
    concatenate x1, other arithmetic, on_device(): full_vals = jnp.concatenate([windows[:, :, 2 * dim:], regs[:, :, dim:]], 1)  3.32 us
  transfers between devices with their start and end apart: 1, of which 0 were waited for; matrix products, arithmetic and copies ran while one was open for 8% of the time, Pallas kernels for 0%

commit v1 on v0

v1 whole, which is shorter than its diff:
```python
import functools
import math

import jax
import jax.numpy as jnp
from jax import lax
from jax.experimental import pallas as pl
from jax.experimental.pallas import tpu as pltpu
from jax.sharding import PartitionSpec as P

HEADS = 16
WIN = 8
REG = 16
LANES = 128

NT = (((1,), (1,)), ((), ()))
TN = (((0,), (0,)), ((), ()))
NN = (((1,), (0,)), ((), ()))


def dot(lhs, rhs, dims=NN):
    return lax.dot_general(lhs, rhs, dims, preferred_element_type=jnp.float32)


def layer_norm(values, gain):
    mean = jnp.mean(values, -1, keepdims=True)
    centred = values - mean
    spread = jnp.mean(centred * centred, -1, keepdims=True)
    return centred * lax.rsqrt(spread + 1e-05) * gain


def head_mask(qlen, hdim):
    per = LANES // hdim
    row = lax.broadcasted_iota(jnp.int32, (per * qlen, LANES), 0) // qlen
    lane = lax.broadcasted_iota(jnp.int32, (per * qlen, LANES), 1) // hdim
    return jnp.where(row == lane, 1.0, 0.0).astype(jnp.bfloat16)


def attend_group(query, keys, values, mask, hdim):
    per = LANES // hdim
    stacked = jnp.concatenate([query] * per, 0) * mask
    scores = dot(keys, stacked, NT)
    top = jnp.max(scores, 0, keepdims=True)
    expo = jnp.exp2((scores - top) * (math.log2(math.e) / math.sqrt(hdim)))
    total = jnp.sum(expo, 0, keepdims=True)
    mixed = dot(values, expo.astype(jnp.bfloat16), TN)
    return mixed * (1.0 / total)


def pick_heads(mixed, qlen, hdim):
    per = LANES // hdim
    return jnp.concatenate(
        [mixed[h * hdim : (h + 1) * hdim, h * qlen : (h + 1) * qlen] for h in range(per)], 0
    )


def block_kernel(x_ref, reg_ref, gain_ref, wqkv_ref, wout_ref, out_ref, kv_ref, rqkv_ref):
    rows, width, dim = x_ref.shape
    hdim = dim // HEADS
    count = width // WIN
    gain = gain_ref[...]
    values = x_ref[...].astype(jnp.float32)
    tokens = jnp.concatenate(
        [values[:, w * WIN : (w + 1) * WIN, :].reshape(rows * WIN, dim) for w in range(count)], 0
    )
    normed = layer_norm(tokens, gain).astype(jnp.bfloat16)
    reg_normed = layer_norm(reg_ref[...], gain).astype(jnp.bfloat16)
    qkv = dot(normed, wqkv_ref[...]).astype(jnp.bfloat16)
    reg_qkv = dot(reg_normed, wqkv_ref[...]).astype(jnp.bfloat16)
    kv_ref[...] = qkv[:, dim:]
    rqkv_ref[...] = reg_qkv
    qlen = rows * WIN
    mask = head_mask(qlen, hdim)
    atts = []
    for w in range(count):
        own = qkv[w * qlen : (w + 1) * qlen]
        parts = []
        for g in range(dim // LANES):
            q0, k0, v0 = (g * LANES + j * dim for j in range(3))
            keys = jnp.concatenate([own[:, k0 : k0 + LANES], reg_qkv[:, k0 : k0 + LANES]], 0)
            vals = jnp.concatenate([own[:, v0 : v0 + LANES], reg_qkv[:, v0 : v0 + LANES]], 0)
            mixed = attend_group(own[:, q0 : q0 + LANES], keys, vals, mask, hdim)
            parts.append(pick_heads(mixed, qlen, hdim))
        atts.append(jnp.concatenate(parts, 0).T.astype(jnp.bfloat16))
    att = jnp.concatenate(atts, 0)
    result = tokens + dot(att, wout_ref[...])
    for w in range(count):
        piece = result[w * qlen : (w + 1) * qlen].reshape(rows, WIN, dim)
        out_ref[:, w * WIN : (w + 1) * WIN, :] = piece.astype(jnp.bfloat16)


def register_kernel(kv_ref, rqkv_ref, reg_ref, gain_ref, wout_ref, out_ref, normed_ref):
    dim = reg_ref.shape[1]
    hdim = dim // HEADS
    rqkv = rqkv_ref[...]
    kv = kv_ref[...]
    mask = head_mask(REG, hdim)
    parts = []
    for g in range(dim // LANES):
        lo = g * LANES
        keys = jnp.concatenate([kv[:, lo : lo + LANES], rqkv[:, dim + lo : dim + lo + LANES]], 0)
        vals = jnp.concatenate(
            [kv[:, dim + lo : dim + lo + LANES], rqkv[:, 2 * dim + lo : 2 * dim + lo + LANES]], 0
        )
        mixed = attend_group(rqkv[:, lo : lo + LANES], keys, vals, mask, hdim)
        parts.append(pick_heads(mixed, REG, hdim))
    att = jnp.concatenate(parts, 0).T.astype(jnp.bfloat16)
    result = reg_ref[...] + dot(att, wout_ref[...])
    out_ref[...] = result
    normed_ref[...] = layer_norm(result, gain_ref[...]).astype(jnp.bfloat16)


def grid_kernel(x_ref, r0, r1, r2, r3, gain_ref, wqkv_ref, wout_ref, out_ref, scratch):
    total, dim = x_ref.shape
    width = total // WIN
    cls = width // WIN
    hdim = dim // HEADS
    qlen = WIN * WIN
    step = 4 if cls % 4 == 0 else 1
    gain = gain_ref[...]
    regs = jnp.concatenate([r0[...], r1[...], r2[...], r3[...]], 0)
    reg_kv = dot(regs, wqkv_ref[:, dim:]).astype(jnp.bfloat16)
    mask = head_mask(qlen, hdim)
    lanes = [slice(g * LANES, (g + 1) * LANES) for g in range(dim // LANES)]
    for g, part in enumerate(lanes):
        scratch[g] = x_ref[:, part].astype(jnp.float32)
    for first in range(0, cls, step):
        starts = [a * width + first + c for c in range(step) for a in range(WIN)]
        tokens = jnp.concatenate(
            [
                jnp.concatenate(
                    [scratch[g, pl.ds(start, WIN, stride=cls), :] for start in starts], 0
                )
                for g in range(len(lanes))
            ],
            1,
        )
        normed = layer_norm(tokens, gain).astype(jnp.bfloat16)
        qkv = dot(normed, wqkv_ref[...]).astype(jnp.bfloat16)
        atts = []
        for c in range(step):
            own = qkv[c * qlen : (c + 1) * qlen]
            parts = []
            for g in range(dim // LANES):
                q0, k0, v0 = (g * LANES + j * dim for j in range(3))
                keys = jnp.concatenate(
                    [own[:, k0 : k0 + LANES], reg_kv[:, k0 - dim : k0 - dim + LANES]], 0
                )
                vals = jnp.concatenate(
                    [own[:, v0 : v0 + LANES], reg_kv[:, v0 - dim : v0 - dim + LANES]], 0
                )
                mixed = attend_group(own[:, q0 : q0 + LANES], keys, vals, mask, hdim)
                parts.append(pick_heads(mixed, qlen, hdim))
            atts.append(jnp.concatenate(parts, 0).T.astype(jnp.bfloat16))
        result = tokens + dot(jnp.concatenate(atts, 0), wout_ref[...])
        for i, start in enumerate(starts):
            for g, part in enumerate(lanes):
                scratch[g, pl.ds(start, WIN, stride=cls), :] = result[i * WIN : (i + 1) * WIN, part]
    for g, part in enumerate(lanes):
        out_ref[:, part] = scratch[g].astype(jnp.bfloat16)


def call(kernel, outs, scratch=(), flops=0):
    return pl.pallas_call(
        kernel,
        out_shape=outs,
        scratch_shapes=list(scratch),
        compiler_params=pltpu.CompilerParams(vmem_limit_bytes=40 << 20),
        cost_estimate=pl.CostEstimate(flops=flops, bytes_accessed=4 << 20, transcendentals=0),
    )


def on_device(patches, registers, gain_one, gain_two, w_qkv_one, w_out_one, w_qkv_two, w_out_two):
    rows, width, dim = patches.shape
    nrow = lax.axis_size("row")
    per_band = nrow // WIN
    count = rows * width
    groups = [[a * per_band + p for a in range(WIN)] for p in range(per_band)]

    def swap(values, bit):
        pairs = [
            (a * per_band + p, (a ^ bit) * per_band + p) for a in range(WIN) for p in range(per_band)
        ]
        return lax.ppermute(values, "row", pairs)

    def exchange(values):
        return lax.all_to_all(
            values, "row", 0, 0, axis_index_groups=groups, tiled=True
        )

    bf16, f32 = jnp.bfloat16, jnp.float32
    shape = jax.ShapeDtypeStruct
    g_one, g_two = gain_one.reshape(1, dim), gain_two.reshape(1, dim)
    block_out, kv, rqkv = call(
        block_kernel,
        (
            shape((rows, width, dim), bf16),
            shape((count, 2 * dim), bf16),
            shape((REG, 3 * dim), bf16),
        ),
        flops=2 * count * dim * 4 * dim,
    )(patches, registers, g_one, w_qkv_one, w_out_one)
    reg_out, r0 = call(
        register_kernel, (shape((REG, dim), f32), shape((REG, dim), bf16)), flops=200_000_000
    )(kv, rqkv, registers, g_two, w_out_one)
    r1 = swap(r0, 1)
    r2 = swap(jnp.concatenate([r0, r1], 0), 2)
    r3 = swap(jnp.concatenate([r0, r1, r2], 0), 4)
    arrived = exchange(block_out)
    finished = call(
        grid_kernel,
        shape((count, dim), bf16),
        [pltpu.VMEM((dim // LANES, count, LANES), f32)],
        flops=2 * count * dim * 6 * dim,
    )(arrived.reshape(count, dim), r0, r1, r2, r3, g_two, w_qkv_two, w_out_two)
    patches_out = exchange(finished.reshape(rows, width, dim))
    return (patches_out, reg_out)


def solution(mesh):
    in_specs = (
        P(("grp", "row"), None, None),
        P(("grp", "row"), None),
        P(),
        P(),
        P(),
        P(),
        P(),
        P(),
    )
    out_specs = (P(("grp", "row"), None, None), P(("grp", "row"), None))
    return jax.shard_map(
        on_device, mesh=mesh, in_specs=in_specs, out_specs=out_specs, check_vma=False
    )
```

time: 104 us -> 51.9 us (0.50)
  blocking collectives: 38.4 us -> 14.6 us
  matrix products: 22.3 us -> 0 us
  local copies, waits for them, and re-layouts: 25.2 us -> 5.55 us
  Pallas kernels: 0 us -> 10.4 us
  other arithmetic: 9.17 us -> 0.01 us
  starting transfers between devices: 7.46 us -> 14.3 us
  waiting for transfers between devices: 0.01 us -> 6.02 us
    all_gather x1 -> x0, blocking collectives: 24.1 us -> none  [on_device(): reg_kv = lax.all_gather(own_kv, 'row', axis=0, tiled=True)]
    dot_general x10 -> x0, matrix products: 14.6 us -> none  [the longest x3 7.81 us: attend(): jnp.einsum('nhqk,nkhe->nqhe', weights, v_heads, preferred_element_type=jn...]
    slice x14 -> x0, local copies, waits for them, and re-layouts: 11.6 us -> none  [the longest x1 1.99 us: on_device(): keys_all[:, :, dim:]]
    pallas_call x0 -> x3, Pallas kernels: none -> 10.4 us  [the longest x1 5.27 us: on_device(): call(grid_kernel, shape((count, dim), bf16), [pltpu.VMEM((dim // LANES, c...]
    sub x3 -> x0, matrix products: 7.69 us -> none  [attend(): expo = jnp.exp(scores - top)]
    ppermute x0 -> x3, starting transfers between devices: none -> 6.94 us  [swap(): return lax.ppermute(values, 'row', pairs)]
    convert_element_type x6 -> x0, local copies, waits for them, and re-layouts: 6.92 us -> none  [attend(): return result.reshape(count, qlen, width).astype(jnp.bfloat16)]
    ppermute x0 -> x3, waiting for transfers between devices: none -> 6.01 us  [swap(): return lax.ppermute(values, 'row', pairs)]
  transfers between devices with their start and end apart: 1 -> 4, of which waited for: 0 -> 3; matrix products, arithmetic and copies ran while one was open for 8% -> 0% of each run, Pallas kernels for 0% -> 4%
where the time goes in v1:
time: 51.9 us; the launch traced here: 51.5 us
  blocking collectives  14.6 us (28%)
  starting transfers between devices  14.3 us (28%)
  Pallas kernels  10.4 us (20%)
  waiting for transfers between devices  6.02 us (12%)
  local copies, waits for them, and re-layouts  5.55 us (11%)
  between operations  0.7 us (1%)
    all_to_all x1, blocking collectives, exchange(): lax.all_to_all(values, 'row', 0, 0, axis_index_groups=groups, tiled=True)  14.6 us
    all_to_all x1, starting transfers between devices, exchange(): lax.all_to_all(values, 'row', 0, 0, axis_index_groups=groups, tiled=True)  7.31 us
    ppermute x3, starting transfers between devices, swap(): return lax.ppermute(values, 'row', pairs)  6.94 us
    ppermute x3, waiting for transfers between devices, swap(): return lax.ppermute(values, 'row', pairs)  6.01 us
    unnamed x21, local copies, waits for them, and re-layouts  5.55 us
    pallas_call x1, Pallas kernels, on_device(): call(grid_kernel, shape((count, dim), bf16), [pltpu.VMEM((dim // LANES, c...  5.27 us
    pallas_call x1, Pallas kernels, on_device(): call(block_kernel, (shape((rows, width, dim), bf16), shape((count, 2 * di...  2.98 us
    pallas_call x1, Pallas kernels, on_device(): call(register_kernel, (shape((REG, dim), f32), shape((REG, dim), bf16)),...  2.13 us
  transfers between devices with their start and end apart: 4, of which 3 were waited for; matrix products, arithmetic and copies ran while one was open for 0% of the time, Pallas kernels for 4%

profile of v1, /device:TPU:0, one launch (start us, length us, event | category | flops | bytes accessed | tf_op | source)
XLA Modules:
  0.0 51.5 jit_solution(9551063563882343028)
XLA Ops:
  0.6 0.0 copy-start
  0.6 1.0 %copy-done = bf16[512,512]{1,0:T(8,128)(2,1)S(1)} copy-done((bf16[512,512]{1,0:T(8,128)(2,1)S(1)}, bf16[512,512]{1,0:T(8,128)(2,1)}, u32[]{:S(2)}) %copy-start) | copy-done | bytes 524312
  1.7 0.0 copy-start.2
  1.7 1.4 %copy-done.2 = bf16[512,1536]{1,0:T(8,128)(2,1)S(1)} copy-done((bf16[512,1536]{1,0:T(8,128)(2,1)S(1)}, bf16[512,1536]{1,0:T(8,128)(2,1)}, u32[]{:S(2)}) %copy-start.2) | copy-done | bytes 1572888
  3.1 0.0 copy-start.3
  3.1 0.9 %copy-done.3 = bf16[8,32,512]{2,1,0:T(8,128)(2,1)S(1)} copy-done((bf16[8,32,512]{2,1,0:T(8,128)(2,1)S(1)}, bf16[8,32,512]{2,1,0:T(8,128)(2,1)}, u32[]{:S(2)}) %copy-start.3) | copy-done | bytes 262168
  4.0 0.0 copy-start.4
  4.0 0.8 %copy-done.4 = f32[16,512]{1,0:T(8,128)S(1)} copy-done((f32[16,512]{1,0:T(8,128)S(1)}, f32[16,512]{1,0:T(8,128)}, u32[]{:S(2)}) %copy-start.4) | copy-done | bytes 32792
  4.8 0.0 copy-start.7
  4.8 0.7 %copy-done.7 = f32[512]{0:T(512)S(1)} copy-done((f32[512]{0:T(512)S(1)}, f32[512]{0:T(512)}, u32[]{:S(2)}) %copy-start.7) | copy-done | bytes 2072
  5.5 0.0 copy-start.1
  5.5 0.0 copy-start.5
  5.5 0.0 copy-start.6
  5.5 0.0 copy-start.8
  5.5 0.0 copy-start.9
  5.5 3.0 %shard_map.95 = (bf16[8,32,512]{2,1,0:T(8,128)(2,1)}, bf16[256,1024]{1,0:T(8,128)(2,1)S(1)}, bf16[16,1536]{1,0:T(8,128)(2,1)S(1)}) custom-call(bf16[8,32,512]{2,1,0:T(8,128)(2,1)S(1)} %copy-done.3, f32[16,512]{1,0:T(8,128)S(1)} %copy-done.4, f32[1,512]{1,0:T(1,128)S(1)} %bitcast.8, bf16[512,1536]{1,0:T(8,128)(2,1)S(1)} %copy-done.2, bf16[512,512]{1,0:T(8,128)(2,1)S(1)} %copy-done), custom_call_target="tpu_custom_call" | custom-call | flops 536870912 | bytes 4194304 | tf_op jit(solution)/shard_map/pallas_call | solution.py:194
  8.5 7.3 %all-to-all-start = ((bf16[8,32,512]{2,1,0:T(8,128)(2,1)}), bf16[8,32,512]{2,1,0:T(8,128)(2,1)S(1)}, u32[]{:S(2)}, u32[]{:S(2)}) async-start(bf16[8,32,512]{2,1,0:T(8,128)(2,1)} %get-tuple-element.7), calls=%async_computation | async-start | bytes 524288 | tf_op jit(solution)/shard_map/all_to_all | solution.py:187
  15.8 0.0 copy-done.1
  15.8 0.0 copy-done.5
  15.8 0.0 copy-done.6
  15.8 2.1 %shard_map.96 = (f32[16,512]{1,0:T(8,128)}, bf16[16,512]{1,0:T(8,128)(2,1)S(1)}) custom-call(bf16[256,1024]{1,0:T(8,128)(2,1)S(1)} %get-tuple-element.8.kv_ref, bf16[16,1536]{1,0:T(8,128)(2,1)S(1)} %get-tuple-element.9.rqkv_ref, f32[16,512]{1,0:T(8,128)S(1)} %copy-done.5, f32[1,512]{1,0:T(1,128)S(1)} %bitcast.6, bf16[512,512]{1,0:T(8,128)(2,1)S(1)} %copy-done.1), custom_call_target="tpu_custom_call" | custom-call | flops 200000000 | bytes 4194304 | tf_op jit(solution)/shard_map/pallas_call | solution.py:203
  17.9 2.0 %collective-permute-start = (bf16[16,512]{1,0:T(8,128)(2,1)S(1)}, bf16[16,512]{1,0:T(8,128)(2,1)S(1)}, u32[]{:S(2)}, u32[]{:S(2)}) collective-permute-start(bf16[16,512]{1,0:T(8,128)(2,1)S(1)} %get-tuple-element.10.r0), channel_id=1, source_target_pairs={{0,2},{1,3},{2,0},{3,1},{4,6},{5,7},{6,4},{7,5},{8,10},{9,11},{10,... | collective-permute-start | bytes 49160 | tf_op jit(solution)/shard_map/ppermute | solution.py:184
  20.0 1.7 %collective-permute-done.r1 = bf16[16,512]{1,0:T(8,128)(2,1)S(1)} collective-permute-done((bf16[16,512]{1,0:T(8,128)(2,1)S(1)}, bf16[16,512]{1,0:T(8,128)(2,1)S(1)}, u32[]{:S(2)}, u32[]{:S(2)}) %collective-permute-start) | collective-permute-done | bytes 16416 | tf_op jit(solution)/shard_map/ppermute | solution.py:184
  21.7 2.1 %collective-permute-start.1 = (bf16[32,512]{1,0:T(8,128)(2,1)S(1)}, bf16[32,512]{1,0:T(8,128)(2,1)S(1)}, u32[]{:S(2)}, u32[]{:S(2)}) collective-permute-start(bf16[32,512]{1,0:T(8,128)(2,1)S(1)} %pad_maximum_fusion.1), channel_id=1, source_target_pairs={{0,4},{1,5},{2,6},{3,7},{4,0},{5,1},{6,2},{7,3},{8,12},{9,13},{10,... | collective-permute-start | bytes 98312 | tf_op jit(solution)/shard_map/ppermute | solution.py:184
  23.8 1.9 %collective-permute-done.1.r2 = bf16[32,512]{1,0:T(8,128)(2,1)S(1)} collective-permute-done((bf16[32,512]{1,0:T(8,128)(2,1)S(1)}, bf16[32,512]{1,0:T(8,128)(2,1)S(1)}, u32[]{:S(2)}, u32[]{:S(2)}) %collective-permute-start.1) | collective-permute-done | bytes 32800 | tf_op jit(solution)/shard_map/ppermute | solution.py:184
  25.7 2.8 %collective-permute-start.2 = (bf16[64,512]{1,0:T(8,128)(2,1)S(1)}, bf16[64,512]{1,0:T(8,128)(2,1)S(1)}, u32[]{:S(2)}, u32[]{:S(2)}) collective-permute-start(bf16[64,512]{1,0:T(8,128)(2,1)S(1)} %pad_maximum_fusion), channel_id=1, source_target_pairs={{0,8},{1,9},{2,10},{3,11},{4,12},{5,13},{6,14},{7,15},{8,0},{9,1},... | collective-permute-start | bytes 196616 | tf_op jit(solution)/shard_map/ppermute | solution.py:184
  28.5 2.4 %collective-permute-done.2.r3 = bf16[64,512]{1,0:T(8,128)(2,1)S(1)} collective-permute-done((bf16[64,512]{1,0:T(8,128)(2,1)S(1)}, bf16[64,512]{1,0:T(8,128)(2,1)S(1)}, u32[]{:S(2)}, u32[]{:S(2)}) %collective-permute-start.2) | collective-permute-done | bytes 65568 | tf_op jit(solution)/shard_map/ppermute | solution.py:184
  30.9 0.0 all-to-all-done
  30.9 0.0 copy-done.8
  30.9 0.0 copy-done.9
  30.9 5.3 %shard_map.97 = bf16[256,512]{1,0:T(8,128)(2,1)S(1)} custom-call(bf16[256,512]{1,0:T(8,128)(2,1)S(1)} %bitcast.4, bf16[16,512]{1,0:T(8,128)(2,1)S(1)} %get-tuple-element.10.r0, bf16[16,512]{1,0:T(8,128)(2,1)S(1)} %collective-permute-done.r1, bf16[32,512]{1,0:T(8,128)(2,1)S(1)} %collective-permute-done.1.r2, bf16[64,512]{1,0:T(8,128)(2,1)S(1)} %collective-permute-done.2.r3, ...), custom_call_target="tpu_custom_call" | custom-call | flops 805306368 | bytes 4194304 | tf_op jit(solution)/shard_map/pallas_call | solution.py:210
  36.2 14.6 %all_to_all.10 = bf16[8,32,512]{2,1,0:T(8,128)(2,1)S(1)} all-to-all(bf16[8,32,512]{2,1,0:T(8,128)(2,1)S(1)} %bitcast.5), channel_id=1, replica_groups={{0,2,4,6,8,10,12,14},{1,3,5,7,9,11,13,15},{16,18,20,22,24,26,28,30},{17..., dimensions={0} | all-to-all | bytes 524288 | tf_op jit(solution)/shard_map/all_to_all | solution.py:187
  50.8 0.7 %copy.11 = bf16[8,32,512]{2,1,0:T(8,128)(2,1)} copy(bf16[8,32,512]{2,1,0:T(8,128)(2,1)S(1)} %all_to_all.10) | data formatting | bytes 524288
  (2 shorter events, 0.0 us)
Async XLA Ops:
  0.6 1.0 %copy-start = (bf16[512,512]{1,0:T(8,128)(2,1)S(1)}, bf16[512,512]{1,0:T(8,128)(2,1)}, u32[]{:S(2)}) copy-start(bf16[512,512]{1,0:T(8,128)(2,1)} %wout_ref.4) | copy-start | bytes 1572868
  1.7 1.4 %copy-start.2 = (bf16[512,1536]{1,0:T(8,128)(2,1)S(1)}, bf16[512,1536]{1,0:T(8,128)(2,1)}, u32[]{:S(2)}) copy-start(bf16[512,1536]{1,0:T(8,128)(2,1)} %wqkv_ref.2) | copy-start | bytes 4718596
  3.1 0.9 %copy-start.3 = (bf16[8,32,512]{2,1,0:T(8,128)(2,1)S(1)}, bf16[8,32,512]{2,1,0:T(8,128)(2,1)}, u32[]{:S(2)}) copy-start(bf16[8,32,512]{2,1,0:T(8,128)(2,1)} %x_ref.1) | copy-start | bytes 786436
  4.0 0.8 %copy-start.4 = (f32[16,512]{1,0:T(8,128)S(1)}, f32[16,512]{1,0:T(8,128)}, u32[]{:S(2)}) copy-start(f32[16,512]{1,0:T(8,128)} %reg_ref.3) | copy-start | bytes 98308
  4.8 0.7 %copy-start.7 = (f32[512]{0:T(512)S(1)}, f32[512]{0:T(512)}, u32[]{:S(2)}) copy-start(f32[512]{0:T(512)} %param.10) | copy-start | bytes 6148
  5.5 10.3 %copy-start.1 = (bf16[512,512]{1,0:T(8,128)(2,1)S(1)}, bf16[512,512]{1,0:T(8,128)(2,1)}, u32[]{:S(2)}) copy-start(bf16[512,512]{1,0:T(8,128)(2,1)} %wout_ref.4) | copy-start | bytes 1572868
  5.5 10.3 %copy-start.5 = (f32[16,512]{1,0:T(8,128)S(1)}, f32[16,512]{1,0:T(8,128)}, u32[]{:S(2)}) copy-start(f32[16,512]{1,0:T(8,128)} %reg_ref.3) | copy-start | bytes 98308
  5.5 10.3 %copy-start.6 = (f32[512]{0:T(512)S(1)}, f32[512]{0:T(512)}, u32[]{:S(2)}) copy-start(f32[512]{0:T(512)} %param.11) | copy-start | bytes 6148
  5.5 25.4 %copy-start.8 = (bf16[512,1536]{1,0:T(8,128)(2,1)S(1)}, bf16[512,1536]{1,0:T(8,128)(2,1)}, u32[]{:S(2)}) copy-start(bf16[512,1536]{1,0:T(8,128)(2,1)} %wqkv_ref.3) | copy-start | bytes 4718596
  5.5 25.4 %copy-start.9 = (bf16[512,512]{1,0:T(8,128)(2,1)S(1)}, bf16[512,512]{1,0:T(8,128)(2,1)}, u32[]{:S(2)}) copy-start(bf16[512,512]{1,0:T(8,128)(2,1)} %wout_ref.5) | copy-start | bytes 1572868
  8.5 22.4 %all-to-all-start = ((bf16[8,32,512]{2,1,0:T(8,128)(2,1)}), bf16[8,32,512]{2,1,0:T(8,128)(2,1)S(1)}, u32[]{:S(2)}, u32[]{:S(2)}) async-start(bf16[8,32,512]{2,1,0:T(8,128)(2,1)} %get-tuple-element.7), calls=%async_computation | async-start | bytes 524288 | tf_op jit(solution)/shard_map/all_to_all | solution.py:187
  17.9 3.8 %collective-permute-start = (bf16[16,512]{1,0:T(8,128)(2,1)S(1)}, bf16[16,512]{1,0:T(8,128)(2,1)S(1)}, u32[]{:S(2)}, u32[]{:S(2)}) collective-permute-start(bf16[16,512]{1,0:T(8,128)(2,1)S(1)} %get-tuple-element.10.r0), channel_id=1, source_target_pairs={{0,2},{1,3},{2,0},{3,1},{4,6},{5,7},{6,4},{7,5},{8,10},{9,11},{10,... | collective-permute-start | bytes 49160 | tf_op jit(solution)/shard_map/ppermute | solution.py:184
  21.7 4.0 %collective-permute-start.1 = (bf16[32,512]{1,0:T(8,128)(2,1)S(1)}, bf16[32,512]{1,0:T(8,128)(2,1)S(1)}, u32[]{:S(2)}, u32[]{:S(2)}) collective-permute-start(bf16[32,512]{1,0:T(8,128)(2,1)S(1)} %pad_maximum_fusion.1), channel_id=1, source_target_pairs={{0,4},{1,5},{2,6},{3,7},{4,0},{5,1},{6,2},{7,3},{8,12},{9,13},{10,... | collective-permute-start | bytes 98312 | tf_op jit(solution)/shard_map/ppermute | solution.py:184
  25.7 5.2 %collective-permute-start.2 = (bf16[64,512]{1,0:T(8,128)(2,1)S(1)}, bf16[64,512]{1,0:T(8,128)(2,1)S(1)}, u32[]{:S(2)}, u32[]{:S(2)}) collective-permute-start(bf16[64,512]{1,0:T(8,128)(2,1)S(1)} %pad_maximum_fusion), channel_id=1, source_target_pairs={{0,8},{1,9},{2,10},{3,11},{4,12},{5,13},{6,14},{7,15},{8,0},{9,1},... | collective-permute-start | bytes 196616 | tf_op jit(solution)/shard_map/ppermute | solution.py:184

commit v2 on v1

--- a/solution.py
+++ b/solution.py
@@ -54,7 +54,40 @@
     )
 
 
-def block_kernel(x_ref, reg_ref, gain_ref, wqkv_ref, wout_ref, out_ref, kv_ref, rqkv_ref):
+def register_attention(query, keys, values, hdim):
+    dim = query.shape[1]
+    mask = head_mask(REG, hdim)
+    per = LANES // hdim
+    scores = []
+    for lo in range(0, dim, LANES):
+        stacked = jnp.concatenate([query[:, lo : lo + LANES]] * per, 0) * mask
+        scores.append(dot(keys[:, lo : lo + LANES], stacked, NT))
+    scores = jnp.concatenate(scores, 1)
+    top = jnp.max(scores, 0, keepdims=True)
+    expo = jnp.exp2((scores - top) * (math.log2(math.e) / math.sqrt(hdim)))
+    weights = (expo * (1.0 / jnp.sum(expo, 0, keepdims=True))).astype(jnp.bfloat16)
+    mixed = dot(weights, values, TN)
+    lane = lax.broadcasted_iota(jnp.int32, (REG, dim), 1) // hdim
+    result = jnp.zeros((REG, dim), jnp.float32)
+    for h in range(HEADS):
+        result = jnp.where(lane == h, mixed[h * REG : (h + 1) * REG], result)
+    return result.astype(jnp.bfloat16)
+
+
+def block_kernel(
+    x_hbm, reg_hbm, gain_hbm, gain_two_hbm, wqkv_hbm, wout_hbm,
+    out_ref, reg_out_ref,
+    x_ref, reg_ref, gain_ref, gain_two_ref, wqkv_ref, wout_ref, sems,
+):
+    pairs = [
+        (x_hbm, x_ref), (reg_hbm, reg_ref), (gain_hbm, gain_ref),
+        (wqkv_hbm, wqkv_ref), (wout_hbm, wout_ref), (gain_two_hbm, gain_two_ref),
+    ]
+    copies = [pltpu.make_async_copy(src, dst, sems.at[i]) for i, (src, dst) in enumerate(pairs)]
+    for copy in copies:
+        copy.start()
+    for copy in copies[:3]:
+        copy.wait()
     rows, width, dim = x_ref.shape
     hdim = dim // HEADS
     count = width // WIN
@@ -65,10 +98,22 @@
     )
     normed = layer_norm(tokens, gain).astype(jnp.bfloat16)
     reg_normed = layer_norm(reg_ref[...], gain).astype(jnp.bfloat16)
+    copies[3].wait()
     qkv = dot(normed, wqkv_ref[...]).astype(jnp.bfloat16)
     reg_qkv = dot(reg_normed, wqkv_ref[...]).astype(jnp.bfloat16)
-    kv_ref[...] = qkv[:, dim:]
-    rqkv_ref[...] = reg_qkv
+    reg_att = register_attention(
+        reg_qkv[:, :dim],
+        jnp.concatenate([qkv[:, dim : 2 * dim], reg_qkv[:, dim : 2 * dim]], 0),
+        jnp.concatenate([qkv[:, 2 * dim :], reg_qkv[:, 2 * dim :]], 0),
+        hdim,
+    )
+    copies[4].wait()
+    copies[5].wait()
+    reg_out = reg_ref[...] + dot(reg_att, wout_ref[...])
+    reg_out_ref[...] = reg_out
+    travelling = layer_norm(reg_out, gain_two_ref[...]).astype(jnp.bfloat16)
+    for r in range(rows):
+        out_ref[r, width:, :] = travelling
     qlen = rows * WIN
     mask = head_mask(qlen, hdim)
     atts = []
@@ -89,41 +134,20 @@
         out_ref[:, w * WIN : (w + 1) * WIN, :] = piece.astype(jnp.bfloat16)
 
 
-def register_kernel(kv_ref, rqkv_ref, reg_ref, gain_ref, wout_ref, out_ref, normed_ref):
-    dim = reg_ref.shape[1]
-    hdim = dim // HEADS
-    rqkv = rqkv_ref[...]
-    kv = kv_ref[...]
-    mask = head_mask(REG, hdim)
-    parts = []
-    for g in range(dim // LANES):
-        lo = g * LANES
-        keys = jnp.concatenate([kv[:, lo : lo + LANES], rqkv[:, dim + lo : dim + lo + LANES]], 0)
-        vals = jnp.concatenate(
-            [kv[:, dim + lo : dim + lo + LANES], rqkv[:, 2 * dim + lo : 2 * dim + lo + LANES]], 0
-        )
-        mixed = attend_group(rqkv[:, lo : lo + LANES], keys, vals, mask, hdim)
-        parts.append(pick_heads(mixed, REG, hdim))
-    att = jnp.concatenate(parts, 0).T.astype(jnp.bfloat16)
-    result = reg_ref[...] + dot(att, wout_ref[...])
-    out_ref[...] = result
-    normed_ref[...] = layer_norm(result, gain_ref[...]).astype(jnp.bfloat16)
-
-
-def grid_kernel(x_ref, r0, r1, r2, r3, gain_ref, wqkv_ref, wout_ref, out_ref, scratch):
-    total, dim = x_ref.shape
-    width = total // WIN
+def grid_kernel(x_ref, gain_ref, wqkv_ref, wout_ref, out_ref, scratch):
+    _, width, dim = out_ref.shape
     cls = width // WIN
     hdim = dim // HEADS
     qlen = WIN * WIN
     step = 4 if cls % 4 == 0 else 1
     gain = gain_ref[...]
-    regs = jnp.concatenate([r0[...], r1[...], r2[...], r3[...]], 0)
+    regs = jnp.concatenate([x_ref[a, width:, :] for a in range(WIN)], 0)
     reg_kv = dot(regs, wqkv_ref[:, dim:]).astype(jnp.bfloat16)
     mask = head_mask(qlen, hdim)
     lanes = [slice(g * LANES, (g + 1) * LANES) for g in range(dim // LANES)]
     for g, part in enumerate(lanes):
-        scratch[g] = x_ref[:, part].astype(jnp.float32)
+        for a in range(WIN):
+            scratch[g, a * width : (a + 1) * width] = x_ref[a, :width, part].astype(jnp.float32)
     for first in range(0, cls, step):
         starts = [a * width + first + c for c in range(step) for a in range(WIN)]
         tokens = jnp.concatenate(
@@ -157,16 +181,19 @@
             for g, part in enumerate(lanes):
                 scratch[g, pl.ds(start, WIN, stride=cls), :] = result[i * WIN : (i + 1) * WIN, part]
     for g, part in enumerate(lanes):
-        out_ref[:, part] = scratch[g].astype(jnp.bfloat16)
-
-
-def call(kernel, outs, scratch=(), flops=0):
+        for a in range(WIN):
+            out_ref[a, :, part] = scratch[g, a * width : (a + 1) * width].astype(jnp.bfloat16)
+
+
+def call(kernel, outs, scratch=(), flops=0, in_specs=None):
+    specs = {} if in_specs is None else {"in_specs": in_specs}
     return pl.pallas_call(
         kernel,
         out_shape=outs,
         scratch_shapes=list(scratch),
         compiler_params=pltpu.CompilerParams(vmem_limit_bytes=40 << 20),
         cost_estimate=pl.CostEstimate(flops=flops, bytes_accessed=4 << 20, transcendentals=0),
+        **specs,
     )
 
 
@@ -177,12 +204,6 @@
     count = rows * width
     groups = [[a * per_band + p for a in range(WIN)] for p in range(per_band)]
 
-    def swap(values, bit):
-        pairs = [
-            (a * per_band + p, (a ^ bit) * per_band + p) for a in range(WIN) for p in range(per_band)
-        ]
-        return lax.ppermute(values, "row", pairs)
-
     def exchange(values):
         return lax.all_to_all(
             values, "row", 0, 0, axis_index_groups=groups, tiled=True
@@ -191,29 +212,32 @@
     bf16, f32 = jnp.bfloat16, jnp.float32
     shape = jax.ShapeDtypeStruct
     g_one, g_two = gain_one.reshape(1, dim), gain_two.reshape(1, dim)
-    block_out, kv, rqkv = call(
+    fetched = [
+        pltpu.with_memory_space_constraint(value, pltpu.MemorySpace.HBM)
+        for value in (patches, registers, g_one, g_two, w_qkv_one, w_out_one)
+    ]
+    outgoing, reg_out = call(
         block_kernel,
-        (
-            shape((rows, width, dim), bf16),
-            shape((count, 2 * dim), bf16),
-            shape((REG, 3 * dim), bf16),
-        ),
+        (shape((rows, width + REG, dim), bf16), shape((REG, dim), f32)),
+        [
+            pltpu.VMEM((rows, width, dim), bf16),
+            pltpu.VMEM((REG, dim), f32),
+            pltpu.VMEM((1, dim), f32),
+            pltpu.VMEM((1, dim), f32),
+            pltpu.VMEM((dim, 3 * dim), bf16),
+            pltpu.VMEM((dim, dim), bf16),
+            pltpu.SemaphoreType.DMA((6,)),
+        ],
         flops=2 * count * dim * 4 * dim,
-    )(patches, registers, g_one, w_qkv_one, w_out_one)
-    reg_out, r0 = call(
-        register_kernel, (shape((REG, dim), f32), shape((REG, dim), bf16)), flops=200_000_000
-    )(kv, rqkv, registers, g_two, w_out_one)
-    r1 = swap(r0, 1)
-    r2 = swap(jnp.concatenate([r0, r1], 0), 2)
-    r3 = swap(jnp.concatenate([r0, r1, r2], 0), 4)
-    arrived = exchange(block_out)
+        in_specs=[pl.BlockSpec(memory_space=pltpu.MemorySpace.HBM)] * 6,
+    )(*fetched)
     finished = call(
         grid_kernel,
-        shape((count, dim), bf16),
+        shape((rows, width, dim), bf16),
         [pltpu.VMEM((dim // LANES, count, LANES), f32)],
         flops=2 * count * dim * 6 * dim,
-    )(arrived.reshape(count, dim), r0, r1, r2, r3, g_two, w_qkv_two, w_out_two)
-    patches_out = exchange(finished.reshape(rows, width, dim))
+    )(exchange(outgoing), g_two, w_qkv_two, w_out_two)
+    patches_out = exchange(finished)
     return (patches_out, reg_out)
 
 

time: 51.9 us -> 42.4 us (0.82)
  blocking collectives: 14.6 us -> 30.9 us
  starting transfers between devices: 14.3 us -> 0 us
  waiting for transfers between devices: 6.02 us -> 0 us
  local copies, waits for them, and re-layouts: 5.55 us -> 0.72 us
    all_to_all x1 -> x2, blocking collectives: 14.6 us -> 30.9 us  [exchange(): lax.all_to_all(values, 'row', 0, 0, axis_index_groups=groups, tiled=True)]
    all_to_all x1 -> x0, starting transfers between devices: 7.31 us -> none  [exchange(): lax.all_to_all(values, 'row', 0, 0, axis_index_groups=groups, tiled=True)]
    ppermute x3 -> x0, starting transfers between devices: 6.94 us -> none  [swap(): return lax.ppermute(values, 'row', pairs)]
    ppermute x3 -> x0, waiting for transfers between devices: 6.01 us -> none  [swap(): return lax.ppermute(values, 'row', pairs)]
    unnamed x21 -> x7, local copies, waits for them, and re-layouts: 5.55 us -> 0.72 us
    pallas_call x3 -> x2, Pallas kernels: 10.4 us -> 9.9 us  [the longest x1 5.3 us: on_device(): call(grid_kernel, shape((rows, width, dim), bf16), [pltpu.VMEM((dim // LA...]
  transfers between devices with their start and end apart: 4 -> 0, of which waited for: 3 -> 0; matrix products, arithmetic and copies ran while one was open for 0% -> 0% of each run, Pallas kernels for 4% -> 0%
where the time goes in v2:
time: 42.4 us; the launch traced here: 42.2 us
  blocking collectives  30.9 us (73%)
  Pallas kernels  9.9 us (23%)
  local copies, waits for them, and re-layouts  0.72 us (2%)
  between operations  0.68 us (2%)
    all_to_all x2, blocking collectives, exchange(): lax.all_to_all(values, 'row', 0, 0, axis_index_groups=groups, tiled=True)  30.9 us
    pallas_call x1, Pallas kernels, on_device(): call(grid_kernel, shape((rows, width, dim), bf16), [pltpu.VMEM((dim // LA...  5.3 us
    pallas_call x1, Pallas kernels, on_device(): call(block_kernel, (shape((rows, width + REG, dim), bf16), shape((REG, di...  4.6 us

profile of v2, /device:TPU:0, one launch (start us, length us, event | category | flops | bytes accessed | tf_op | source)
XLA Modules:
  0.0 42.2 jit_solution(61840687121120018)
XLA Ops:
  0.6 0.0 copy-start
  0.6 0.0 copy-start.1
  0.7 0.0 copy-start.2
  0.7 4.6 %shard_map.95 = (bf16[8,48,512]{2,1,0:T(8,128)(2,1)S(1)}, f32[16,512]{1,0:T(8,128)}) custom-call(bf16[8,32,512]{2,1,0:T(8,128)(2,1)} %x_hbm.1, f32[16,512]{1,0:T(8,128)} %reg_hbm.1, f32[1,512]{1,0:T(1,128)} %bitcast.4, f32[1,512]{1,0:T(1,128)} %bitcast.2, bf16[512,1536]{1,0:T(8,128)(2,1)} %wqkv_hbm.1, bf16[512,512]{1,0:T(8,128)(2,1)} %wout_hbm.1), custom_call_target="tpu_custom_call" | custom-call | flops 536870912 | bytes 4194304 | tf_op jit(solution)/shard_map/pallas_call | solution.py:219
  5.3 19.2 %all_to_all.10.x_ref = bf16[8,48,512]{2,1,0:T(8,128)(2,1)S(1)} all-to-all(bf16[8,48,512]{2,1,0:T(8,128)(2,1)S(1)} %get-tuple-element.4), channel_id=1, replica_groups={{0,2,4,6,8,10,12,14},{1,3,5,7,9,11,13,15},{16,18,20,22,24,26,28,30},{17..., dimensions={0} | all-to-all | bytes 786432 | tf_op jit(solution)/shard_map/all_to_all | solution.py:208
  24.4 0.0 copy-done
  24.4 0.0 copy-done.1
  24.4 0.0 copy-done.2
  24.4 5.3 %shard_map.96 = bf16[8,32,512]{2,1,0:T(8,128)(2,1)S(1)} custom-call(bf16[8,48,512]{2,1,0:T(8,128)(2,1)S(1)} %all_to_all.10.x_ref, f32[1,512]{1,0:T(1,128)S(1)} %bitcast.3, bf16[512,1536]{1,0:T(8,128)(2,1)S(1)} %copy-done.1, bf16[512,512]{1,0:T(8,128)(2,1)S(1)} %copy-done.2), custom_call_target="tpu_custom_call" | custom-call | flops 805306368 | bytes 4194304 | tf_op jit(solution)/shard_map/pallas_call | solution.py:234
  29.7 11.8 %all_to_all.11 = bf16[8,32,512]{2,1,0:T(8,128)(2,1)S(1)} all-to-all(bf16[8,32,512]{2,1,0:T(8,128)(2,1)S(1)} %shard_map.96), channel_id=1, replica_groups={{0,2,4,6,8,10,12,14},{1,3,5,7,9,11,13,15},{16,18,20,22,24,26,28,30},{17..., dimensions={0} | all-to-all | bytes 524288 | tf_op jit(solution)/shard_map/all_to_all | solution.py:208
  41.5 0.7 %copy.11 = bf16[8,32,512]{2,1,0:T(8,128)(2,1)} copy(bf16[8,32,512]{2,1,0:T(8,128)(2,1)S(1)} %all_to_all.11) | data formatting | bytes 524288
Async XLA Ops:
  0.6 23.8 %copy-start = (f32[512]{0:T(512)S(1)}, f32[512]{0:T(512)}, u32[]{:S(2)}) copy-start(f32[512]{0:T(512)} %param.11) | copy-start | bytes 6148
  0.6 23.8 %copy-start.1 = (bf16[512,1536]{1,0:T(8,128)(2,1)S(1)}, bf16[512,1536]{1,0:T(8,128)(2,1)}, u32[]{:S(2)}) copy-start(bf16[512,1536]{1,0:T(8,128)(2,1)} %wqkv_ref.1) | copy-start | bytes 4718596
  0.7 23.8 %copy-start.2 = (bf16[512,512]{1,0:T(8,128)(2,1)S(1)}, bf16[512,512]{1,0:T(8,128)(2,1)}, u32[]{:S(2)}) copy-start(bf16[512,512]{1,0:T(8,128)(2,1)} %wout_ref.1) | copy-start | bytes 1572868

commit v3 on v2

--- a/solution.py
+++ b/solution.py
@@ -36,22 +36,54 @@
     return jnp.where(row == lane, 1.0, 0.0).astype(jnp.bfloat16)
 
 
-def attend_group(query, keys, values, mask, hdim):
-    per = LANES // hdim
-    stacked = jnp.concatenate([query] * per, 0) * mask
-    scores = dot(keys, stacked, NT)
-    top = jnp.max(scores, 0, keepdims=True)
-    expo = jnp.exp2((scores - top) * (math.log2(math.e) / math.sqrt(hdim)))
-    total = jnp.sum(expo, 0, keepdims=True)
-    mixed = dot(values, expo.astype(jnp.bfloat16), TN)
-    return mixed * (1.0 / total)
-
-
 def pick_heads(mixed, qlen, hdim):
-    per = LANES // hdim
     return jnp.concatenate(
-        [mixed[h * hdim : (h + 1) * hdim, h * qlen : (h + 1) * qlen] for h in range(per)], 0
-    )
+        [
+            mixed[h * hdim : (h + 1) * hdim, h * qlen : (h + 1) * qlen]
+            for h in range(LANES // hdim)
+        ],
+        0,
+    )
+
+
+def attend_windows(qkv, reg_keys, reg_values, windows, qlen, mask, hdim):
+    dim = reg_keys.shape[1]
+    units = [(w, slice(lo, lo + LANES)) for w in windows for lo in range(0, dim, LANES)]
+    tops, totals, done, held, weights = {}, {}, {}, {}, {}
+
+    def scores(n):
+        w, part = units[n]
+        own = qkv[w * qlen : (w + 1) * qlen]
+        keys = jnp.concatenate([own[:, dim : 2 * dim][:, part], reg_keys[:, part]], 0)
+        stacked = jnp.concatenate([own[:, part]] * (LANES // hdim), 0) * mask
+        result = dot(keys, stacked, NT)
+        held[n] = result
+        tops[n] = jnp.max(result, 0, keepdims=True)
+
+    def exponentials(n):
+        scale = math.log2(math.e) / math.sqrt(hdim)
+        expo = jnp.exp2((held.pop(n) - tops[n]) * scale)
+        totals[n] = 1.0 / jnp.sum(expo, 0, keepdims=True)
+        weights[n] = expo.astype(jnp.bfloat16)
+
+    def weighted(n):
+        w, part = units[n]
+        own = qkv[w * qlen : (w + 1) * qlen]
+        values = jnp.concatenate([own[:, 2 * dim :][:, part], reg_values[:, part]], 0)
+        mixed = dot(values, weights.pop(n), TN) * totals[n]
+        done[n] = pick_heads(mixed, qlen, hdim)
+
+    for n in range(len(units) + 8):
+        if n < len(units):
+            scores(n)
+        if 0 <= n - 4 < len(units):
+            exponentials(n - 4)
+        if 0 <= n - 8:
+            weighted(n - 8)
+    per = dim // LANES
+    return [
+        jnp.concatenate([done[i * per + g] for g in range(per)], 0) for i in range(len(windows))
+    ]
 
 
 def register_attention(query, keys, values, hdim):
@@ -98,7 +130,8 @@
     )
     normed = layer_norm(tokens, gain).astype(jnp.bfloat16)
     reg_normed = layer_norm(reg_ref[...], gain).astype(jnp.bfloat16)
-    copies[3].wait()
+    for copy in copies[3:]:
+        copy.wait()
     qkv = dot(normed, wqkv_ref[...]).astype(jnp.bfloat16)
     reg_qkv = dot(reg_normed, wqkv_ref[...]).astype(jnp.bfloat16)
     reg_att = register_attention(
@@ -107,8 +140,6 @@
         jnp.concatenate([qkv[:, 2 * dim :], reg_qkv[:, 2 * dim :]], 0),
         hdim,
     )
-    copies[4].wait()
-    copies[5].wait()
     reg_out = reg_ref[...] + dot(reg_att, wout_ref[...])
     reg_out_ref[...] = reg_out
     travelling = layer_norm(reg_out, gain_two_ref[...]).astype(jnp.bfloat16)
@@ -116,18 +147,11 @@
         out_ref[r, width:, :] = travelling
     qlen = rows * WIN
     mask = head_mask(qlen, hdim)
-    atts = []
-    for w in range(count):
-        own = qkv[w * qlen : (w + 1) * qlen]
-        parts = []
-        for g in range(dim // LANES):
-            q0, k0, v0 = (g * LANES + j * dim for j in range(3))
-            keys = jnp.concatenate([own[:, k0 : k0 + LANES], reg_qkv[:, k0 : k0 + LANES]], 0)
-            vals = jnp.concatenate([own[:, v0 : v0 + LANES], reg_qkv[:, v0 : v0 + LANES]], 0)
-            mixed = attend_group(own[:, q0 : q0 + LANES], keys, vals, mask, hdim)
-            parts.append(pick_heads(mixed, qlen, hdim))
-        atts.append(jnp.concatenate(parts, 0).T.astype(jnp.bfloat16))
-    att = jnp.concatenate(atts, 0)
+    reg_keys, reg_values = reg_qkv[:, dim : 2 * dim], reg_qkv[:, 2 * dim :]
+    atts = attend_windows(
+        qkv, reg_keys, reg_values, range(count), qlen, mask, hdim
+    )
+    att = jnp.concatenate([each.T.astype(jnp.bfloat16) for each in atts], 0)
     result = tokens + dot(att, wout_ref[...])
     for w in range(count):
         piece = result[w * qlen : (w + 1) * qlen].reshape(rows, WIN, dim)
@@ -161,22 +185,11 @@
         )
         normed = layer_norm(tokens, gain).astype(jnp.bfloat16)
         qkv = dot(normed, wqkv_ref[...]).astype(jnp.bfloat16)
-        atts = []
-        for c in range(step):
-            own = qkv[c * qlen : (c + 1) * qlen]
-            parts = []
-            for g in range(dim // LANES):
-                q0, k0, v0 = (g * LANES + j * dim for j in range(3))
-                keys = jnp.concatenate(
-                    [own[:, k0 : k0 + LANES], reg_kv[:, k0 - dim : k0 - dim + LANES]], 0
-                )
-                vals = jnp.concatenate(
-                    [own[:, v0 : v0 + LANES], reg_kv[:, v0 - dim : v0 - dim + LANES]], 0
-                )
-                mixed = attend_group(own[:, q0 : q0 + LANES], keys, vals, mask, hdim)
-                parts.append(pick_heads(mixed, qlen, hdim))
-            atts.append(jnp.concatenate(parts, 0).T.astype(jnp.bfloat16))
-        result = tokens + dot(jnp.concatenate(atts, 0), wout_ref[...])
+        atts = attend_windows(
+            qkv, reg_kv[:, :dim], reg_kv[:, dim:], range(step), qlen, mask, hdim
+        )
+        att = jnp.concatenate([each.T.astype(jnp.bfloat16) for each in atts], 0)
+        result = tokens + dot(att, wout_ref[...])
         for i, start in enumerate(starts):
             for g, part in enumerate(lanes):
                 scratch[g, pl.ds(start, WIN, stride=cls), :] = result[i * WIN : (i + 1) * WIN, part]
@@ -234,7 +247,9 @@
     finished = call(
         grid_kernel,
         shape((rows, width, dim), bf16),
-        [pltpu.VMEM((dim // LANES, count, LANES), f32)],
+        [
+            pltpu.VMEM((dim // LANES, count, LANES), f32),
+        ],
         flops=2 * count * dim * 6 * dim,
     )(exchange(outgoing), g_two, w_qkv_two, w_out_two)
     patches_out = exchange(finished)

time: 42.4 us -> 39.1 us (0.922)
  Pallas kernels: 9.9 us -> 6.56 us
    pallas_call x1, Pallas kernels: 5.3 us -> 2.17 us  [on_device(): call(grid_kernel, shape((rows, width, dim), bf16), [pltpu.VMEM((dim // LA...]
where the time goes in v3:
time: 39.1 us; the launch traced here: 38.9 us
  blocking collectives  31 us (79%)
  Pallas kernels  6.56 us (17%)
  local copies, waits for them, and re-layouts  0.72 us (2%)
  between operations  0.68 us (2%)
    all_to_all x2, blocking collectives, exchange(): lax.all_to_all(values, 'row', 0, 0, axis_index_groups=groups, tiled=True)  31 us
    pallas_call x1, Pallas kernels, on_device(): call(block_kernel, (shape((rows, width + REG, dim), bf16), shape((REG, di...  4.39 us
    pallas_call x1, Pallas kernels, on_device(): call(grid_kernel, shape((rows, width, dim), bf16), [pltpu.VMEM((dim // LA...  2.17 us

profile of v3, /device:TPU:0, one launch (start us, length us, event | category | flops | bytes accessed | tf_op | source)
XLA Modules:
  0.0 38.9 jit_solution(11357261444644473889)
XLA Ops:
  0.6 0.0 copy-start
  0.6 0.0 copy-start.1
  0.7 0.0 copy-start.2
  0.7 4.4 %shard_map.95 = (bf16[8,48,512]{2,1,0:T(8,128)(2,1)S(1)}, f32[16,512]{1,0:T(8,128)}) custom-call(bf16[8,32,512]{2,1,0:T(8,128)(2,1)} %x_hbm.1, f32[16,512]{1,0:T(8,128)} %reg_hbm.1, f32[1,512]{1,0:T(1,128)} %bitcast.4, f32[1,512]{1,0:T(1,128)} %bitcast.2, bf16[512,1536]{1,0:T(8,128)(2,1)} %wqkv_hbm.1, bf16[512,512]{1,0:T(8,128)(2,1)} %wout_hbm.1), custom_call_target="tpu_custom_call" | custom-call | flops 536870912 | bytes 4194304 | tf_op jit(solution)/shard_map/pallas_call | solution.py:232
  5.1 19.2 %all_to_all.10.x_ref = bf16[8,48,512]{2,1,0:T(8,128)(2,1)S(1)} all-to-all(bf16[8,48,512]{2,1,0:T(8,128)(2,1)S(1)} %get-tuple-element.4), channel_id=1, replica_groups={{0,2,4,6,8,10,12,14},{1,3,5,7,9,11,13,15},{16,18,20,22,24,26,28,30},{17..., dimensions={0} | all-to-all | bytes 786432 | tf_op jit(solution)/shard_map/all_to_all | solution.py:221
  24.2 0.0 copy-done
  24.2 0.0 copy-done.1
  24.2 0.0 copy-done.2
  24.2 2.2 %shard_map.96 = bf16[8,32,512]{2,1,0:T(8,128)(2,1)S(1)} custom-call(bf16[8,48,512]{2,1,0:T(8,128)(2,1)S(1)} %all_to_all.10.x_ref, f32[1,512]{1,0:T(1,128)S(1)} %bitcast.3, bf16[512,1536]{1,0:T(8,128)(2,1)S(1)} %copy-done.1, bf16[512,512]{1,0:T(8,128)(2,1)S(1)} %copy-done.2), custom_call_target="tpu_custom_call" | custom-call | flops 805306368 | bytes 4194304 | tf_op jit(solution)/shard_map/pallas_call | solution.py:247
  26.4 11.8 %all_to_all.11 = bf16[8,32,512]{2,1,0:T(8,128)(2,1)S(1)} all-to-all(bf16[8,32,512]{2,1,0:T(8,128)(2,1)S(1)} %shard_map.96), channel_id=1, replica_groups={{0,2,4,6,8,10,12,14},{1,3,5,7,9,11,13,15},{16,18,20,22,24,26,28,30},{17..., dimensions={0} | all-to-all | bytes 524288 | tf_op jit(solution)/shard_map/all_to_all | solution.py:221
  38.2 0.7 %copy.11 = bf16[8,32,512]{2,1,0:T(8,128)(2,1)} copy(bf16[8,32,512]{2,1,0:T(8,128)(2,1)S(1)} %all_to_all.11) | data formatting | bytes 524288
Async XLA Ops:
  0.6 23.6 %copy-start = (f32[512]{0:T(512)S(1)}, f32[512]{0:T(512)}, u32[]{:S(2)}) copy-start(f32[512]{0:T(512)} %param.11) | copy-start | bytes 6148
  0.6 23.6 %copy-start.1 = (bf16[512,1536]{1,0:T(8,128)(2,1)S(1)}, bf16[512,1536]{1,0:T(8,128)(2,1)}, u32[]{:S(2)}) copy-start(bf16[512,1536]{1,0:T(8,128)(2,1)} %wqkv_ref.1) | copy-start | bytes 4718596
  0.7 23.6 %copy-start.2 = (bf16[512,512]{1,0:T(8,128)(2,1)S(1)}, bf16[512,512]{1,0:T(8,128)(2,1)}, u32[]{:S(2)}) copy-start(bf16[512,512]{1,0:T(8,128)(2,1)} %wout_ref.1) | copy-start | bytes 1572868

commit v4 on v3

--- a/solution.py
+++ b/solution.py
@@ -12,6 +12,7 @@
 WIN = 8
 REG = 16
 LANES = 128
+ORDER = (5, 4, 1, 0, 7, 6, 3, 2)
 
 NT = (((1,), (1,)), ((), ()))
 TN = (((0,), (0,)), ((), ()))
@@ -215,7 +216,7 @@
     nrow = lax.axis_size("row")
     per_band = nrow // WIN
     count = rows * width
-    groups = [[a * per_band + p for a in range(WIN)] for p in range(per_band)]
+    groups = [[a * per_band + p for a in ORDER] for p in range(per_band)]
 
     def exchange(values):
         return lax.all_to_all(

time: 39.1 us -> 34.1 us (0.87)
  blocking collectives: 31 us -> 25.9 us
    all_to_all x2, blocking collectives: 31 us -> 25.9 us  [exchange(): lax.all_to_all(values, 'row', 0, 0, axis_index_groups=groups, tiled=True)]
where the time goes in v4:
time: 34.1 us; the launch traced here: 33.8 us
  blocking collectives  25.9 us (76%)
  Pallas kernels  6.55 us (19%)
  local copies, waits for them, and re-layouts  0.72 us (2%)
  between operations  0.68 us (2%)
    all_to_all x2, blocking collectives, exchange(): lax.all_to_all(values, 'row', 0, 0, axis_index_groups=groups, tiled=True)  25.9 us
    pallas_call x1, Pallas kernels, on_device(): call(block_kernel, (shape((rows, width + REG, dim), bf16), shape((REG, di...  4.39 us
    pallas_call x1, Pallas kernels, on_device(): call(grid_kernel, shape((rows, width, dim), bf16), [pltpu.VMEM((dim // LA...  2.16 us
    unnamed x7, local copies, waits for them, and re-layouts  0.72 us

profile of v4, /device:TPU:0, one launch (start us, length us, event | category | flops | bytes accessed | tf_op | source)
XLA Modules:
  0.0 33.8 jit_solution(12290099471872227813)
XLA Ops:
  0.6 0.0 copy-start
  0.6 0.0 copy-start.1
  0.7 0.0 copy-start.2
  0.7 4.4 %shard_map.95 = (bf16[8,48,512]{2,1,0:T(8,128)(2,1)S(1)}, f32[16,512]{1,0:T(8,128)}) custom-call(bf16[8,32,512]{2,1,0:T(8,128)(2,1)} %x_hbm.1, f32[16,512]{1,0:T(8,128)} %reg_hbm.1, f32[1,512]{1,0:T(1,128)} %bitcast.4, f32[1,512]{1,0:T(1,128)} %bitcast.2, bf16[512,1536]{1,0:T(8,128)(2,1)} %wqkv_hbm.1, bf16[512,512]{1,0:T(8,128)(2,1)} %wout_hbm.1), custom_call_target="tpu_custom_call" | custom-call | flops 536870912 | bytes 4194304 | tf_op jit(solution)/shard_map/pallas_call | solution.py:233
  5.1 16.6 %all_to_all.10.x_ref = bf16[8,48,512]{2,1,0:T(8,128)(2,1)S(1)} all-to-all(bf16[8,48,512]{2,1,0:T(8,128)(2,1)S(1)} %get-tuple-element.4), channel_id=1, replica_groups={{10,8,2,0,14,12,6,4},{11,9,3,1,15,13,7,5},{26,24,18,16,30,28,22,20},{27..., dimensions={0} | all-to-all | bytes 786432 | tf_op jit(solution)/shard_map/all_to_all | solution.py:222
  21.7 0.0 copy-done
  21.7 0.0 copy-done.1
  21.7 0.0 copy-done.2
  21.7 2.2 %shard_map.96 = bf16[8,32,512]{2,1,0:T(8,128)(2,1)S(1)} custom-call(bf16[8,48,512]{2,1,0:T(8,128)(2,1)S(1)} %all_to_all.10.x_ref, f32[1,512]{1,0:T(1,128)S(1)} %bitcast.3, bf16[512,1536]{1,0:T(8,128)(2,1)S(1)} %copy-done.1, bf16[512,512]{1,0:T(8,128)(2,1)S(1)} %copy-done.2), custom_call_target="tpu_custom_call" | custom-call | flops 805306368 | bytes 4194304 | tf_op jit(solution)/shard_map/pallas_call | solution.py:248
  23.9 9.3 %all_to_all.11 = bf16[8,32,512]{2,1,0:T(8,128)(2,1)S(1)} all-to-all(bf16[8,32,512]{2,1,0:T(8,128)(2,1)S(1)} %shard_map.96), channel_id=1, replica_groups={{10,8,2,0,14,12,6,4},{11,9,3,1,15,13,7,5},{26,24,18,16,30,28,22,20},{27..., dimensions={0} | all-to-all | bytes 524288 | tf_op jit(solution)/shard_map/all_to_all | solution.py:222
  33.1 0.7 %copy.11 = bf16[8,32,512]{2,1,0:T(8,128)(2,1)} copy(bf16[8,32,512]{2,1,0:T(8,128)(2,1)S(1)} %all_to_all.11) | data formatting | bytes 524288
Async XLA Ops:
  0.6 21.1 %copy-start = (f32[512]{0:T(512)S(1)}, f32[512]{0:T(512)}, u32[]{:S(2)}) copy-start(f32[512]{0:T(512)} %param.11) | copy-start | bytes 6148
  0.6 21.1 %copy-start.1 = (bf16[512,1536]{1,0:T(8,128)(2,1)S(1)}, bf16[512,1536]{1,0:T(8,128)(2,1)}, u32[]{:S(2)}) copy-start(bf16[512,1536]{1,0:T(8,128)(2,1)} %wqkv_ref.1) | copy-start | bytes 4718596
  0.7 21.1 %copy-start.2 = (bf16[512,512]{1,0:T(8,128)(2,1)S(1)}, bf16[512,512]{1,0:T(8,128)(2,1)}, u32[]{:S(2)}) copy-start(bf16[512,512]{1,0:T(8,128)(2,1)} %wout_ref.1) | copy-start | bytes 1572868

commit v5 on v4

--- a/solution.py
+++ b/solution.py
@@ -12,6 +12,8 @@
 WIN = 8
 REG = 16
 LANES = 128
+STAGE_AT = (0, 6, 10, 14)
+BLOCK_GAPS, GRID_GAPS = (4, 8), (4, 8)
 ORDER = (5, 4, 1, 0, 7, 6, 3, 2)
 
 NT = (((1,), (1,)), ((), ()))
@@ -47,7 +49,7 @@
     )
 
 
-def attend_windows(qkv, reg_keys, reg_values, windows, qlen, mask, hdim):
+def attend_windows(qkv, reg_keys, reg_values, windows, qlen, mask, hdim, gaps, beside={}):
     dim = reg_keys.shape[1]
     units = [(w, slice(lo, lo + LANES)) for w in windows for lo in range(0, dim, LANES)]
     tops, totals, done, held, weights = {}, {}, {}, {}, {}
@@ -74,47 +76,63 @@
         mixed = dot(values, weights.pop(n), TN) * totals[n]
         done[n] = pick_heads(mixed, qlen, hdim)
 
-    for n in range(len(units) + 8):
+    to_expo, to_mixed = gaps
+    for n in range(len(units) + to_mixed):
         if n < len(units):
             scores(n)
-        if 0 <= n - 4 < len(units):
-            exponentials(n - 4)
-        if 0 <= n - 8:
-            weighted(n - 8)
+        if 0 <= n - to_expo < len(units):
+            exponentials(n - to_expo)
+        if 0 <= n - to_mixed:
+            weighted(n - to_mixed)
+        if n in beside:
+            beside[n]()
     per = dim // LANES
     return [
         jnp.concatenate([done[i * per + g] for g in range(per)], 0) for i in range(len(windows))
     ]
 
 
-def register_attention(query, keys, values, hdim):
+def register_stages(query, keys, values, hdim, finish):
     dim = query.shape[1]
-    mask = head_mask(REG, hdim)
-    per = LANES // hdim
-    scores = []
-    for lo in range(0, dim, LANES):
-        stacked = jnp.concatenate([query[:, lo : lo + LANES]] * per, 0) * mask
-        scores.append(dot(keys[:, lo : lo + LANES], stacked, NT))
-    scores = jnp.concatenate(scores, 1)
-    top = jnp.max(scores, 0, keepdims=True)
-    expo = jnp.exp2((scores - top) * (math.log2(math.e) / math.sqrt(hdim)))
-    weights = (expo * (1.0 / jnp.sum(expo, 0, keepdims=True))).astype(jnp.bfloat16)
-    mixed = dot(weights, values, TN)
-    lane = lax.broadcasted_iota(jnp.int32, (REG, dim), 1) // hdim
-    result = jnp.zeros((REG, dim), jnp.float32)
-    for h in range(HEADS):
-        result = jnp.where(lane == h, mixed[h * REG : (h + 1) * REG], result)
-    return result.astype(jnp.bfloat16)
+    held = {}
+
+    def scores():
+        mask = head_mask(REG, hdim)
+        per = LANES // hdim
+        parts = []
+        for lo in range(0, dim, LANES):
+            stacked = jnp.concatenate([query[:, lo : lo + LANES]] * per, 0) * mask
+            parts.append(dot(keys[:, lo : lo + LANES], stacked, NT))
+        held["scores"] = jnp.concatenate(parts, 1)
+
+    def weights():
+        top = jnp.max(held["scores"], 0, keepdims=True)
+        scale = math.log2(math.e) / math.sqrt(hdim)
+        expo = jnp.exp2((held.pop("scores") - top) * scale)
+        held["weights"] = (expo * (1.0 / jnp.sum(expo, 0, keepdims=True))).astype(jnp.bfloat16)
+
+    def mixed():
+        result = dot(held.pop("weights"), values, TN)
+        lane = lax.broadcasted_iota(jnp.int32, (REG, dim), 1) // hdim
+        picked = jnp.zeros((REG, dim), jnp.float32)
+        for h in range(HEADS):
+            picked = jnp.where(lane == h, result[h * REG : (h + 1) * REG], picked)
+        held["picked"] = picked.astype(jnp.bfloat16)
+
+    return [scores, weights, mixed, lambda: finish(held["picked"])]
 
 
 def block_kernel(
     x_hbm, reg_hbm, gain_hbm, gain_two_hbm, wqkv_hbm, wout_hbm,
-    out_ref, reg_out_ref,
-    x_ref, reg_ref, gain_ref, gain_two_ref, wqkv_ref, wout_ref, sems,
+    out_ref, reg_out_hbm,
+    reg_out_ref, x_ref, reg_ref, gain_ref, gain_two_ref, wqkv_ref, wout_ref, sems,
 ):
+    dim = x_ref.shape[2]
+    thirds = [slice(j * dim, (j + 1) * dim) for j in range(3)]
     pairs = [
         (x_hbm, x_ref), (reg_hbm, reg_ref), (gain_hbm, gain_ref),
-        (wqkv_hbm, wqkv_ref), (wout_hbm, wout_ref), (gain_two_hbm, gain_two_ref),
+        *((wqkv_hbm.at[:, part], wqkv_ref.at[:, part]) for part in thirds),
+        (wout_hbm, wout_ref), (gain_two_hbm, gain_two_ref),
     ]
     copies = [pltpu.make_async_copy(src, dst, sems.at[i]) for i, (src, dst) in enumerate(pairs)]
     for copy in copies:
@@ -131,32 +149,45 @@
     )
     normed = layer_norm(tokens, gain).astype(jnp.bfloat16)
     reg_normed = layer_norm(reg_ref[...], gain).astype(jnp.bfloat16)
-    for copy in copies[3:]:
+    both = []
+    everything = jnp.concatenate([normed, reg_normed], 0)
+    for part, copy in zip(thirds, copies[3:6]):
         copy.wait()
-    qkv = dot(normed, wqkv_ref[...]).astype(jnp.bfloat16)
-    reg_qkv = dot(reg_normed, wqkv_ref[...]).astype(jnp.bfloat16)
-    reg_att = register_attention(
+        both.append(dot(everything, wqkv_ref[:, part]).astype(jnp.bfloat16))
+    both = jnp.concatenate(both, 1)
+    qkv, reg_qkv = both[: rows * width], both[rows * width :]
+    for copy in copies[6:]:
+        copy.wait()
+
+    leaving = pltpu.make_async_copy(reg_out_ref, reg_out_hbm, sems.at[8])
+
+    def finish(reg_att):
+        reg_out = reg_ref[...] + dot(reg_att, wout_ref[...])
+        reg_out_ref[...] = reg_out
+        leaving.start()
+        travelling = layer_norm(reg_out, gain_two_ref[...]).astype(jnp.bfloat16)
+        for r in range(rows):
+            out_ref[r, width:, :] = travelling
+
+    stages = register_stages(
         reg_qkv[:, :dim],
         jnp.concatenate([qkv[:, dim : 2 * dim], reg_qkv[:, dim : 2 * dim]], 0),
         jnp.concatenate([qkv[:, 2 * dim :], reg_qkv[:, 2 * dim :]], 0),
         hdim,
-    )
-    reg_out = reg_ref[...] + dot(reg_att, wout_ref[...])
-    reg_out_ref[...] = reg_out
-    travelling = layer_norm(reg_out, gain_two_ref[...]).astype(jnp.bfloat16)
-    for r in range(rows):
-        out_ref[r, width:, :] = travelling
+        finish,
+    )
     qlen = rows * WIN
     mask = head_mask(qlen, hdim)
     reg_keys, reg_values = reg_qkv[:, dim : 2 * dim], reg_qkv[:, 2 * dim :]
     atts = attend_windows(
-        qkv, reg_keys, reg_values, range(count), qlen, mask, hdim
+        qkv, reg_keys, reg_values, range(count), qlen, mask, hdim, BLOCK_GAPS, dict(zip(STAGE_AT, stages))
     )
     att = jnp.concatenate([each.T.astype(jnp.bfloat16) for each in atts], 0)
     result = tokens + dot(att, wout_ref[...])
     for w in range(count):
         piece = result[w * qlen : (w + 1) * qlen].reshape(rows, WIN, dim)
         out_ref[:, w * WIN : (w + 1) * WIN, :] = piece.astype(jnp.bfloat16)
+    leaving.wait()
 
 
 def grid_kernel(x_ref, gain_ref, wqkv_ref, wout_ref, out_ref, scratch):
@@ -187,7 +218,7 @@
         normed = layer_norm(tokens, gain).astype(jnp.bfloat16)
         qkv = dot(normed, wqkv_ref[...]).astype(jnp.bfloat16)
         atts = attend_windows(
-            qkv, reg_kv[:, :dim], reg_kv[:, dim:], range(step), qlen, mask, hdim
+            qkv, reg_kv[:, :dim], reg_kv[:, dim:], range(step), qlen, mask, hdim, GRID_GAPS
         )
         att = jnp.concatenate([each.T.astype(jnp.bfloat16) for each in atts], 0)
         result = tokens + dot(att, wout_ref[...])
@@ -199,8 +230,7 @@
             out_ref[a, :, part] = scratch[g, a * width : (a + 1) * width].astype(jnp.bfloat16)
 
 
-def call(kernel, outs, scratch=(), flops=0, in_specs=None):
-    specs = {} if in_specs is None else {"in_specs": in_specs}
+def call(kernel, outs, scratch=(), flops=0, **specs):
     return pl.pallas_call(
         kernel,
         out_shape=outs,
@@ -234,16 +264,21 @@
         block_kernel,
         (shape((rows, width + REG, dim), bf16), shape((REG, dim), f32)),
         [
+            pltpu.VMEM((REG, dim), f32),
             pltpu.VMEM((rows, width, dim), bf16),
             pltpu.VMEM((REG, dim), f32),
             pltpu.VMEM((1, dim), f32),
             pltpu.VMEM((1, dim), f32),
             pltpu.VMEM((dim, 3 * dim), bf16),
             pltpu.VMEM((dim, dim), bf16),
-            pltpu.SemaphoreType.DMA((6,)),
+            pltpu.SemaphoreType.DMA((9,)),
         ],
         flops=2 * count * dim * 4 * dim,
         in_specs=[pl.BlockSpec(memory_space=pltpu.MemorySpace.HBM)] * 6,
+        out_specs=(
+            pl.BlockSpec(memory_space=pltpu.MemorySpace.VMEM),
+            pl.BlockSpec(memory_space=pltpu.MemorySpace.HBM),
+        ),
     )(*fetched)
     finished = call(
         grid_kernel,

time: 34.1 us -> 33.7 us (0.988)
  Pallas kernels: 6.55 us -> 6.14 us
    pallas_call x1, Pallas kernels: 4.39 us -> 3.98 us  [on_device(): call(block_kernel, (shape((rows, width + REG, dim), bf16), shape((REG, di...]
where the time goes in v5:
time: 33.7 us; the launch traced here: 33.4 us
  blocking collectives  25.9 us (77%)
  Pallas kernels  6.14 us (18%)
  local copies, waits for them, and re-layouts  0.72 us (2%)
  between operations  0.68 us (2%)
    all_to_all x2, blocking collectives, exchange(): lax.all_to_all(values, 'row', 0, 0, axis_index_groups=groups, tiled=True)  25.9 us
    pallas_call x1, Pallas kernels, on_device(): call(block_kernel, (shape((rows, width + REG, dim), bf16), shape((REG, di...  3.98 us
    pallas_call x1, Pallas kernels, on_device(): call(grid_kernel, shape((rows, width, dim), bf16), [pltpu.VMEM((dim // LA...  2.16 us
    unnamed x7, local copies, waits for them, and re-layouts  0.72 us

profile of v5, /device:TPU:0, one launch (start us, length us, event | category | flops | bytes accessed | tf_op | source)
XLA Modules:
  0.0 33.4 jit_solution(4313768864646025916)
XLA Ops:
  0.6 0.0 copy-start
  0.6 0.0 copy-start.1
  0.7 0.0 copy-start.2
  0.7 4.0 %shard_map.95 = (bf16[8,48,512]{2,1,0:T(8,128)(2,1)S(1)}, f32[16,512]{1,0:T(8,128)}) custom-call(bf16[8,32,512]{2,1,0:T(8,128)(2,1)} %x_hbm.1, f32[16,512]{1,0:T(8,128)} %reg_hbm.1, f32[1,512]{1,0:T(1,128)} %bitcast.4, f32[1,512]{1,0:T(1,128)} %bitcast.2, bf16[512,1536]{1,0:T(8,128)(2,1)} %wqkv_hbm.1, bf16[512,512]{1,0:T(8,128)(2,1)} %wout_hbm.1), custom_call_target="tpu_custom_call" | custom-call | flops 536870912 | bytes 4194304 | tf_op jit(solution)/shard_map/pallas_call | solution.py:263
  4.7 16.6 %all_to_all.10.x_ref = bf16[8,48,512]{2,1,0:T(8,128)(2,1)S(1)} all-to-all(bf16[8,48,512]{2,1,0:T(8,128)(2,1)S(1)} %get-tuple-element.4), channel_id=1, replica_groups={{10,8,2,0,14,12,6,4},{11,9,3,1,15,13,7,5},{26,24,18,16,30,28,22,20},{27..., dimensions={0} | all-to-all | bytes 786432 | tf_op jit(solution)/shard_map/all_to_all | solution.py:252
  21.3 0.0 copy-done
  21.3 0.0 copy-done.1
  21.3 0.0 copy-done.2
  21.3 2.2 %shard_map.96 = bf16[8,32,512]{2,1,0:T(8,128)(2,1)S(1)} custom-call(bf16[8,48,512]{2,1,0:T(8,128)(2,1)S(1)} %all_to_all.10.x_ref, f32[1,512]{1,0:T(1,128)S(1)} %bitcast.3, bf16[512,1536]{1,0:T(8,128)(2,1)S(1)} %copy-done.1, bf16[512,512]{1,0:T(8,128)(2,1)S(1)} %copy-done.2), custom_call_target="tpu_custom_call" | custom-call | flops 805306368 | bytes 4194304 | tf_op jit(solution)/shard_map/pallas_call | solution.py:283
  23.5 9.3 %all_to_all.11 = bf16[8,32,512]{2,1,0:T(8,128)(2,1)S(1)} all-to-all(bf16[8,32,512]{2,1,0:T(8,128)(2,1)S(1)} %shard_map.96), channel_id=1, replica_groups={{10,8,2,0,14,12,6,4},{11,9,3,1,15,13,7,5},{26,24,18,16,30,28,22,20},{27..., dimensions={0} | all-to-all | bytes 524288 | tf_op jit(solution)/shard_map/all_to_all | solution.py:252
  32.7 0.7 %copy.11 = bf16[8,32,512]{2,1,0:T(8,128)(2,1)} copy(bf16[8,32,512]{2,1,0:T(8,128)(2,1)S(1)} %all_to_all.11) | data formatting | bytes 524288
Async XLA Ops:
  0.6 20.7 %copy-start = (f32[512]{0:T(512)S(1)}, f32[512]{0:T(512)}, u32[]{:S(2)}) copy-start(f32[512]{0:T(512)} %param.11) | copy-start | bytes 6148
  0.6 20.7 %copy-start.1 = (bf16[512,1536]{1,0:T(8,128)(2,1)S(1)}, bf16[512,1536]{1,0:T(8,128)(2,1)}, u32[]{:S(2)}) copy-start(bf16[512,1536]{1,0:T(8,128)(2,1)} %wqkv_ref.1) | copy-start | bytes 4718596
  0.7 20.7 %copy-start.2 = (bf16[512,512]{1,0:T(8,128)(2,1)S(1)}, bf16[512,512]{1,0:T(8,128)(2,1)}, u32[]{:S(2)}) copy-start(bf16[512,512]{1,0:T(8,128)(2,1)} %wout_ref.1) | copy-start | bytes 1572868

commit v6 on v5

--- a/solution.py
+++ b/solution.py
@@ -12,8 +12,8 @@
 WIN = 8
 REG = 16
 LANES = 128
-STAGE_AT = (0, 6, 10, 14)
-BLOCK_GAPS, GRID_GAPS = (4, 8), (4, 8)
+STAGE_AT = (0, 10, 16, 20)
+BLOCK_GAPS, GRID_GAPS = (4, 8), (5, 10)
 ORDER = (5, 4, 1, 0, 7, 6, 3, 2)
 
 NT = (((1,), (1,)), ((), ()))
@@ -30,6 +30,10 @@
     centred = values - mean
     spread = jnp.mean(centred * centred, -1, keepdims=True)
     return centred * lax.rsqrt(spread + 1e-05) * gain
+
+
+def score_scale(hdim):
+    return math.log2(math.e) / math.sqrt(hdim)
 
 
 def head_mask(qlen, hdim):
@@ -64,8 +68,7 @@
         tops[n] = jnp.max(result, 0, keepdims=True)
 
     def exponentials(n):
-        scale = math.log2(math.e) / math.sqrt(hdim)
-        expo = jnp.exp2((held.pop(n) - tops[n]) * scale)
+        expo = jnp.exp2(held.pop(n) - tops[n])
         totals[n] = 1.0 / jnp.sum(expo, 0, keepdims=True)
         weights[n] = expo.astype(jnp.bfloat16)
 
@@ -107,8 +110,7 @@
 
     def weights():
         top = jnp.max(held["scores"], 0, keepdims=True)
-        scale = math.log2(math.e) / math.sqrt(hdim)
-        expo = jnp.exp2((held.pop("scores") - top) * scale)
+        expo = jnp.exp2(held.pop("scores") - top)
         held["weights"] = (expo * (1.0 / jnp.sum(expo, 0, keepdims=True))).astype(jnp.bfloat16)
 
     def mixed():
@@ -128,10 +130,10 @@
     reg_out_ref, x_ref, reg_ref, gain_ref, gain_two_ref, wqkv_ref, wout_ref, sems,
 ):
     dim = x_ref.shape[2]
-    thirds = [slice(j * dim, (j + 1) * dim) for j in range(3)]
+    parts = [slice(0, 2 * dim), slice(2 * dim, 3 * dim)]
     pairs = [
         (x_hbm, x_ref), (reg_hbm, reg_ref), (gain_hbm, gain_ref),
-        *((wqkv_hbm.at[:, part], wqkv_ref.at[:, part]) for part in thirds),
+        *((wqkv_hbm.at[:, part], wqkv_ref.at[:, part]) for part in parts),
         (wout_hbm, wout_ref), (gain_two_hbm, gain_two_ref),
     ]
     copies = [pltpu.make_async_copy(src, dst, sems.at[i]) for i, (src, dst) in enumerate(pairs)]
@@ -149,17 +151,17 @@
     )
     normed = layer_norm(tokens, gain).astype(jnp.bfloat16)
     reg_normed = layer_norm(reg_ref[...], gain).astype(jnp.bfloat16)
-    both = []
     everything = jnp.concatenate([normed, reg_normed], 0)
-    for part, copy in zip(thirds, copies[3:6]):
+    copies[3].wait()
+    early = dot(everything, wqkv_ref[:, parts[0]])
+    early = jnp.concatenate([early[:, :dim] * score_scale(hdim), early[:, dim:]], 1)
+    for copy in copies[4:]:
         copy.wait()
-        both.append(dot(everything, wqkv_ref[:, part]).astype(jnp.bfloat16))
-    both = jnp.concatenate(both, 1)
+    late = dot(everything, wqkv_ref[:, parts[1]])
+    both = jnp.concatenate([early.astype(jnp.bfloat16), late.astype(jnp.bfloat16)], 1)
     qkv, reg_qkv = both[: rows * width], both[rows * width :]
-    for copy in copies[6:]:
-        copy.wait()
-
-    leaving = pltpu.make_async_copy(reg_out_ref, reg_out_hbm, sems.at[8])
+
+    leaving = pltpu.make_async_copy(reg_out_ref, reg_out_hbm, sems.at[7])
 
     def finish(reg_att):
         reg_out = reg_ref[...] + dot(reg_att, wout_ref[...])
@@ -216,7 +218,13 @@
             1,
         )
         normed = layer_norm(tokens, gain).astype(jnp.bfloat16)
-        qkv = dot(normed, wqkv_ref[...]).astype(jnp.bfloat16)
+        qkv = jnp.concatenate(
+            [
+                (dot(normed, wqkv_ref[:, :dim]) * score_scale(hdim)).astype(jnp.bfloat16),
+                dot(normed, wqkv_ref[:, dim:]).astype(jnp.bfloat16),
+            ],
+            1,
+        )
         atts = attend_windows(
             qkv, reg_kv[:, :dim], reg_kv[:, dim:], range(step), qlen, mask, hdim, GRID_GAPS
         )
@@ -271,7 +279,7 @@
             pltpu.VMEM((1, dim), f32),
             pltpu.VMEM((dim, 3 * dim), bf16),
             pltpu.VMEM((dim, dim), bf16),
-            pltpu.SemaphoreType.DMA((9,)),
+            pltpu.SemaphoreType.DMA((8,)),
         ],
         flops=2 * count * dim * 4 * dim,
         in_specs=[pl.BlockSpec(memory_space=pltpu.MemorySpace.HBM)] * 6,

time: 33.7 us -> 33.5 us (level)
  no operation moved by 1% of the time
where the time goes in v6:
time: 33.5 us; the launch traced here: 33.3 us
  blocking collectives  25.9 us (77%)
  Pallas kernels  5.96 us (18%)
  local copies, waits for them, and re-layouts  0.72 us (2%)
  between operations  0.68 us (2%)
    all_to_all x2, blocking collectives, exchange(): lax.all_to_all(values, 'row', 0, 0, axis_index_groups=groups, tiled=True)  25.9 us
    pallas_call x1, Pallas kernels, on_device(): call(block_kernel, (shape((rows, width + REG, dim), bf16), shape((REG, di...  3.87 us
    pallas_call x1, Pallas kernels, on_device(): call(grid_kernel, shape((rows, width, dim), bf16), [pltpu.VMEM((dim // LA...  2.09 us
    unnamed x7, local copies, waits for them, and re-layouts  0.72 us

profile of v6, /device:TPU:0, one launch (start us, length us, event | category | flops | bytes accessed | tf_op | source)
XLA Modules:
  0.0 33.3 jit_solution(17111578233631635215)
XLA Ops:
  0.6 0.0 copy-start
  0.6 0.0 copy-start.1
  0.7 0.0 copy-start.2
  0.7 3.9 %shard_map.95 = (bf16[8,48,512]{2,1,0:T(8,128)(2,1)S(1)}, f32[16,512]{1,0:T(8,128)}) custom-call(bf16[8,32,512]{2,1,0:T(8,128)(2,1)} %x_hbm.1, f32[16,512]{1,0:T(8,128)} %reg_hbm.1, f32[1,512]{1,0:T(1,128)} %bitcast.4, f32[1,512]{1,0:T(1,128)} %bitcast.2, bf16[512,1536]{1,0:T(8,128)(2,1)} %wqkv_hbm.1, bf16[512,512]{1,0:T(8,128)(2,1)} %wout_hbm.1), custom_call_target="tpu_custom_call" | custom-call | flops 536870912 | bytes 4194304 | tf_op jit(solution)/shard_map/pallas_call | solution.py:271
  4.5 16.6 %all_to_all.10.x_ref = bf16[8,48,512]{2,1,0:T(8,128)(2,1)S(1)} all-to-all(bf16[8,48,512]{2,1,0:T(8,128)(2,1)S(1)} %get-tuple-element.4), channel_id=1, replica_groups={{10,8,2,0,14,12,6,4},{11,9,3,1,15,13,7,5},{26,24,18,16,30,28,22,20},{27..., dimensions={0} | all-to-all | bytes 786432 | tf_op jit(solution)/shard_map/all_to_all | solution.py:260
  21.2 0.0 copy-done
  21.2 0.0 copy-done.1
  21.2 0.0 copy-done.2
  21.2 2.1 %shard_map.96 = bf16[8,32,512]{2,1,0:T(8,128)(2,1)S(1)} custom-call(bf16[8,48,512]{2,1,0:T(8,128)(2,1)S(1)} %all_to_all.10.x_ref, f32[1,512]{1,0:T(1,128)S(1)} %bitcast.3, bf16[512,1536]{1,0:T(8,128)(2,1)S(1)} %copy-done.1, bf16[512,512]{1,0:T(8,128)(2,1)S(1)} %copy-done.2), custom_call_target="tpu_custom_call" | custom-call | flops 805306368 | bytes 4194304 | tf_op jit(solution)/shard_map/pallas_call | solution.py:291
  23.3 9.3 %all_to_all.11 = bf16[8,32,512]{2,1,0:T(8,128)(2,1)S(1)} all-to-all(bf16[8,32,512]{2,1,0:T(8,128)(2,1)S(1)} %shard_map.96), channel_id=1, replica_groups={{10,8,2,0,14,12,6,4},{11,9,3,1,15,13,7,5},{26,24,18,16,30,28,22,20},{27..., dimensions={0} | all-to-all | bytes 524288 | tf_op jit(solution)/shard_map/all_to_all | solution.py:260
  32.6 0.7 %copy.11 = bf16[8,32,512]{2,1,0:T(8,128)(2,1)} copy(bf16[8,32,512]{2,1,0:T(8,128)(2,1)S(1)} %all_to_all.11) | data formatting | bytes 524288
Async XLA Ops:
  0.6 20.6 %copy-start = (f32[512]{0:T(512)S(1)}, f32[512]{0:T(512)}, u32[]{:S(2)}) copy-start(f32[512]{0:T(512)} %param.11) | copy-start | bytes 6148
  0.6 20.5 %copy-start.1 = (bf16[512,1536]{1,0:T(8,128)(2,1)S(1)}, bf16[512,1536]{1,0:T(8,128)(2,1)}, u32[]{:S(2)}) copy-start(bf16[512,1536]{1,0:T(8,128)(2,1)} %wqkv_ref.1) | copy-start | bytes 4718596
  0.7 20.5 %copy-start.2 = (bf16[512,512]{1,0:T(8,128)(2,1)S(1)}, bf16[512,512]{1,0:T(8,128)(2,1)}, u32[]{:S(2)}) copy-start(bf16[512,512]{1,0:T(8,128)(2,1)} %wout_ref.1) | copy-start | bytes 1572868

commit v7 on v6

--- a/solution.py
+++ b/solution.py
@@ -14,7 +14,7 @@
 LANES = 128
 STAGE_AT = (0, 10, 16, 20)
 BLOCK_GAPS, GRID_GAPS = (4, 8), (5, 10)
-ORDER = (5, 4, 1, 0, 7, 6, 3, 2)
+ORDER = (5, 4, 3, 0, 7, 6, 1, 2)
 
 NT = (((1,), (1,)), ((), ()))
 TN = (((0,), (0,)), ((), ()))

time: 33.5 us -> 33.4 us (level)
  no operation moved by 1% of the time
where the time goes in v7:
time: 33.4 us; the launch traced here: 33.2 us
  blocking collectives  25.8 us (77%)
  Pallas kernels  5.96 us (18%)
  local copies, waits for them, and re-layouts  0.72 us (2%)
  between operations  0.68 us (2%)
    all_to_all x2, blocking collectives, exchange(): lax.all_to_all(values, 'row', 0, 0, axis_index_groups=groups, tiled=True)  25.8 us
    pallas_call x1, Pallas kernels, on_device(): call(block_kernel, (shape((rows, width + REG, dim), bf16), shape((REG, di...  3.87 us
    pallas_call x1, Pallas kernels, on_device(): call(grid_kernel, shape((rows, width, dim), bf16), [pltpu.VMEM((dim // LA...  2.09 us
    unnamed x7, local copies, waits for them, and re-layouts  0.72 us

profile of v7, /device:TPU:0, one launch (start us, length us, event | category | flops | bytes accessed | tf_op | source)
XLA Modules:
  0.0 33.2 jit_solution(16160480733247680877)
XLA Ops:
  0.6 0.0 copy-start
  0.6 0.0 copy-start.1
  0.7 0.0 copy-start.2
  0.7 3.9 %shard_map.95 = (bf16[8,48,512]{2,1,0:T(8,128)(2,1)S(1)}, f32[16,512]{1,0:T(8,128)}) custom-call(bf16[8,32,512]{2,1,0:T(8,128)(2,1)} %x_hbm.1, f32[16,512]{1,0:T(8,128)} %reg_hbm.1, f32[1,512]{1,0:T(1,128)} %bitcast.4, f32[1,512]{1,0:T(1,128)} %bitcast.2, bf16[512,1536]{1,0:T(8,128)(2,1)} %wqkv_hbm.1, bf16[512,512]{1,0:T(8,128)(2,1)} %wout_hbm.1), custom_call_target="tpu_custom_call" | custom-call | flops 536870912 | bytes 4194304 | tf_op jit(solution)/shard_map/pallas_call | solution.py:271
  4.5 16.6 %all_to_all.10.x_ref = bf16[8,48,512]{2,1,0:T(8,128)(2,1)S(1)} all-to-all(bf16[8,48,512]{2,1,0:T(8,128)(2,1)S(1)} %get-tuple-element.4), channel_id=1, replica_groups={{10,8,6,0,14,12,2,4},{11,9,7,1,15,13,3,5},{26,24,22,16,30,28,18,20},{27..., dimensions={0} | all-to-all | bytes 786432 | tf_op jit(solution)/shard_map/all_to_all | solution.py:260
  21.2 0.0 copy-done
  21.2 0.0 copy-done.1
  21.2 0.0 copy-done.2
  21.2 2.1 %shard_map.96 = bf16[8,32,512]{2,1,0:T(8,128)(2,1)S(1)} custom-call(bf16[8,48,512]{2,1,0:T(8,128)(2,1)S(1)} %all_to_all.10.x_ref, f32[1,512]{1,0:T(1,128)S(1)} %bitcast.3, bf16[512,1536]{1,0:T(8,128)(2,1)S(1)} %copy-done.1, bf16[512,512]{1,0:T(8,128)(2,1)S(1)} %copy-done.2), custom_call_target="tpu_custom_call" | custom-call | flops 805306368 | bytes 4194304 | tf_op jit(solution)/shard_map/pallas_call | solution.py:291
  23.3 9.2 %all_to_all.11 = bf16[8,32,512]{2,1,0:T(8,128)(2,1)S(1)} all-to-all(bf16[8,32,512]{2,1,0:T(8,128)(2,1)S(1)} %shard_map.96), channel_id=1, replica_groups={{10,8,6,0,14,12,2,4},{11,9,7,1,15,13,3,5},{26,24,22,16,30,28,18,20},{27..., dimensions={0} | all-to-all | bytes 524288 | tf_op jit(solution)/shard_map/all_to_all | solution.py:260
  32.5 0.7 %copy.11 = bf16[8,32,512]{2,1,0:T(8,128)(2,1)} copy(bf16[8,32,512]{2,1,0:T(8,128)(2,1)S(1)} %all_to_all.11) | data formatting | bytes 524288
Async XLA Ops:
  0.6 20.6 %copy-start = (f32[512]{0:T(512)S(1)}, f32[512]{0:T(512)}, u32[]{:S(2)}) copy-start(f32[512]{0:T(512)} %param.11) | copy-start | bytes 6148
  0.6 20.5 %copy-start.1 = (bf16[512,1536]{1,0:T(8,128)(2,1)S(1)}, bf16[512,1536]{1,0:T(8,128)(2,1)}, u32[]{:S(2)}) copy-start(bf16[512,1536]{1,0:T(8,128)(2,1)} %wqkv_ref.1) | copy-start | bytes 4718596
  0.7 20.5 %copy-start.2 = (bf16[512,512]{1,0:T(8,128)(2,1)S(1)}, bf16[512,512]{1,0:T(8,128)(2,1)}, u32[]{:S(2)}) copy-start(bf16[512,512]{1,0:T(8,128)(2,1)} %wout_ref.1) | copy-start | bytes 1572868

commit v8 on v6

--- a/solution.py
+++ b/solution.py
@@ -12,8 +12,8 @@
 WIN = 8
 REG = 16
 LANES = 128
-STAGE_AT = (0, 10, 16, 20)
-BLOCK_GAPS, GRID_GAPS = (4, 8), (5, 10)
+STAGE_AT = (0, 8, 14, 18)
+BLOCK_GAPS, GRID_GAPS = (3, 5), (5, 10)
 ORDER = (5, 4, 1, 0, 7, 6, 3, 2)
 
 NT = (((1,), (1,)), ((), ()))

time: 33.5 us -> 33.5 us (level)
  no operation moved by 1% of the time
where the time goes in v8:
time: 33.5 us; the launch traced here: 33.3 us
  blocking collectives  25.9 us (77%)
  Pallas kernels  6 us (18%)
  local copies, waits for them, and re-layouts  0.72 us (2%)
  between operations  0.68 us (2%)
    all_to_all x2, blocking collectives, exchange(): lax.all_to_all(values, 'row', 0, 0, axis_index_groups=groups, tiled=True)  25.9 us
    pallas_call x1, Pallas kernels, on_device(): call(block_kernel, (shape((rows, width + REG, dim), bf16), shape((REG, di...  3.92 us
    pallas_call x1, Pallas kernels, on_device(): call(grid_kernel, shape((rows, width, dim), bf16), [pltpu.VMEM((dim // LA...  2.09 us
    unnamed x7, local copies, waits for them, and re-layouts  0.72 us

profile of v8, /device:TPU:0, one launch (start us, length us, event | category | flops | bytes accessed | tf_op | source)
XLA Modules:
  0.0 33.3 jit_solution(10756913123949873509)
XLA Ops:
  0.6 0.0 copy-start
  0.6 0.0 copy-start.1
  0.7 0.0 copy-start.2
  0.7 3.9 %shard_map.95 = (bf16[8,48,512]{2,1,0:T(8,128)(2,1)S(1)}, f32[16,512]{1,0:T(8,128)}) custom-call(bf16[8,32,512]{2,1,0:T(8,128)(2,1)} %x_hbm.1, f32[16,512]{1,0:T(8,128)} %reg_hbm.1, f32[1,512]{1,0:T(1,128)} %bitcast.4, f32[1,512]{1,0:T(1,128)} %bitcast.2, bf16[512,1536]{1,0:T(8,128)(2,1)} %wqkv_hbm.1, bf16[512,512]{1,0:T(8,128)(2,1)} %wout_hbm.1), custom_call_target="tpu_custom_call" | custom-call | flops 536870912 | bytes 4194304 | tf_op jit(solution)/shard_map/pallas_call | solution.py:271
  4.6 16.6 %all_to_all.10.x_ref = bf16[8,48,512]{2,1,0:T(8,128)(2,1)S(1)} all-to-all(bf16[8,48,512]{2,1,0:T(8,128)(2,1)S(1)} %get-tuple-element.4), channel_id=1, replica_groups={{10,8,2,0,14,12,6,4},{11,9,3,1,15,13,7,5},{26,24,18,16,30,28,22,20},{27..., dimensions={0} | all-to-all | bytes 786432 | tf_op jit(solution)/shard_map/all_to_all | solution.py:260
  21.2 0.0 copy-done
  21.2 0.0 copy-done.1
  21.2 0.0 copy-done.2
  21.2 2.1 %shard_map.96 = bf16[8,32,512]{2,1,0:T(8,128)(2,1)S(1)} custom-call(bf16[8,48,512]{2,1,0:T(8,128)(2,1)S(1)} %all_to_all.10.x_ref, f32[1,512]{1,0:T(1,128)S(1)} %bitcast.3, bf16[512,1536]{1,0:T(8,128)(2,1)S(1)} %copy-done.1, bf16[512,512]{1,0:T(8,128)(2,1)S(1)} %copy-done.2), custom_call_target="tpu_custom_call" | custom-call | flops 805306368 | bytes 4194304 | tf_op jit(solution)/shard_map/pallas_call | solution.py:291
  23.3 9.3 %all_to_all.11 = bf16[8,32,512]{2,1,0:T(8,128)(2,1)S(1)} all-to-all(bf16[8,32,512]{2,1,0:T(8,128)(2,1)S(1)} %shard_map.96), channel_id=1, replica_groups={{10,8,2,0,14,12,6,4},{11,9,3,1,15,13,7,5},{26,24,18,16,30,28,22,20},{27..., dimensions={0} | all-to-all | bytes 524288 | tf_op jit(solution)/shard_map/all_to_all | solution.py:260
  32.6 0.7 %copy.11 = bf16[8,32,512]{2,1,0:T(8,128)(2,1)} copy(bf16[8,32,512]{2,1,0:T(8,128)(2,1)S(1)} %all_to_all.11) | data formatting | bytes 524288
Async XLA Ops:
  0.6 20.6 %copy-start = (f32[512]{0:T(512)S(1)}, f32[512]{0:T(512)}, u32[]{:S(2)}) copy-start(f32[512]{0:T(512)} %param.11) | copy-start | bytes 6148
  0.6 20.6 %copy-start.1 = (bf16[512,1536]{1,0:T(8,128)(2,1)S(1)}, bf16[512,1536]{1,0:T(8,128)(2,1)}, u32[]{:S(2)}) copy-start(bf16[512,1536]{1,0:T(8,128)(2,1)} %wqkv_ref.1) | copy-start | bytes 4718596
  0.7 20.6 %copy-start.2 = (bf16[512,512]{1,0:T(8,128)(2,1)S(1)}, bf16[512,512]{1,0:T(8,128)(2,1)}, u32[]{:S(2)}) copy-start(bf16[512,512]{1,0:T(8,128)(2,1)} %wout_ref.1) | copy-start | bytes 1572868
